TPU v7x, 128 devices: a whole 4x4x4 slice. The times are simulated.
128 devices in a mesh: batch: 16 (over y, z), proto: 8 (over x, core).
Axes of the slice: x: 4, y: 4, z: 4, core: 2. Of those that a mesh axis runs over, the one named last changes fastest.
Arguments:
- embeddings: bfloat16 [16384, 1024], P('batch'), may hold values from -6 to 6
- pairing: int32 [16384], P('batch'), may hold values from 0 to 1023, as said below
- w_in: bfloat16 [1024, 512], replicated, may hold values from -0.1875 to 0.1875
- w_out: bfloat16 [512, 128], replicated, may hold values from -0.25 to 0.25
- prototypes: bfloat16 [32768, 128], P('proto'), may hold values from -1.8 to 1.8
Outputs:
- grad_in: float32 [1024, 512], replicated
- grad_out: float32 [512, 128], replicated
- grad_proto: float32 [32768, 128], P('proto')
Inputs may be any that keep to these rules, and one draw needn't show every extreme that they name: Within every aligned block of 1024 rows the views come in pairs: pairing[pairing[i]] = i and pairing[i] != i, both counted within the block.
All inputs are finite; a program needn't handle non-finite values.
Results may differ from a plain program's by a relative error of at most 0.007.
Values may be sent and summed in bfloat16 or wider, within the bound.
A program may use at most 64 MiB of HBM per device.

v0:
```python
import jax
import jax.numpy as jnp
from jax import lax
from jax.sharding import PartitionSpec as P

ITERS = 3


norm_eps = 1e-06
code_temp = 0.05
pred_temp = 0.1
loss_scale = 64.0


def from_everyone(x, axis):
    copies = jnp.broadcast_to(x, (lax.axis_size(axis), *x.shape))
    return lax.all_to_all(copies, axis, split_axis=0, concat_axis=0, tiled=True)


def of_everyone(x, axis):
    everything = from_everyone(x, axis)
    return jnp.sum(everything, axis=0)


def total_of_pieces(x, axis):
    return lax.all_gather(x, axis).sum(0)


def head_forward(rows_in, w_in, w_out):
    pre_act = jnp.dot(rows_in, w_in, preferred_element_type=jnp.float32)
    hidden = jax.nn.gelu(pre_act).astype(jnp.bfloat16)
    raw_out = jnp.dot(hidden, w_out, preferred_element_type=jnp.float32)
    inv_norm = lax.rsqrt(jnp.sum(raw_out * raw_out, axis=1, keepdims=True) + norm_eps)
    return (pre_act, hidden, raw_out, inv_norm, (raw_out * inv_norm).astype(jnp.bfloat16))


def head_backward(rows_in, w_out, pre_act, hidden, raw_out, inv_norm, view_grad):
    along = jnp.sum(raw_out * view_grad, axis=1, keepdims=True)
    d_raw = (inv_norm * view_grad - raw_out * (inv_norm * inv_norm * inv_norm) * along).astype(
        jnp.bfloat16
    )
    grad_out = lax.dot_general(
        hidden, d_raw, (((0,), (0,)), ((), ())), preferred_element_type=jnp.float32
    )
    d_hidden = lax.dot_general(
        d_raw, w_out, (((1,), (1,)), ((), ())), preferred_element_type=jnp.float32
    )
    _, pullback = jax.vjp(jax.nn.gelu, pre_act)
    d_pre = pullback(d_hidden)[0].astype(jnp.bfloat16)
    grad_in = lax.dot_general(
        rows_in, d_pre, (((0,), (0,)), ((), ())), preferred_element_type=jnp.float32
    )
    return (grad_in, grad_out)


def unit_rows(prototypes):
    proto_f = prototypes.astype(jnp.float32)
    proto_inv = lax.rsqrt(jnp.sum(proto_f * proto_f, axis=1, keepdims=True) + norm_eps)
    return (proto_f, proto_inv, (proto_f * proto_inv).astype(jnp.bfloat16))


def scores_of(rows_in, unit):
    return lax.dot_general(
        rows_in, unit, (((1,), (1,)), ((), ())), preferred_element_type=jnp.float32
    )


def body(embeddings, pairing, w_in, w_out, prototypes):
    proto_f, proto_inv, unit = unit_rows(prototypes)
    width = unit.shape[0]
    depth = unit.shape[1]
    block_cols = min(1024, width)
    count = width // block_cols
    unit_blocks = unit.reshape(count, block_cols, depth)
    rows = embeddings.shape[0]
    pre_act, hidden, raw_out, inv_norm, views = head_forward(embeddings, w_in, w_out)
    mates = views[pairing]
    row_scale = jnp.ones((rows,), jnp.float32)
    col_scale = jnp.ones((width,), jnp.float32)
    totals = jnp.ones((rows,), jnp.float32)
    for sweep in range(ITERS):

        def one_block(block):
            return jnp.sum(
                row_scale[:, None] * jnp.exp(scores_of(views, block) / code_temp), axis=0
            )

        column_partial_value = lax.map(one_block, unit_blocks).reshape(width)
        col_scale = 1.0 / of_everyone(column_partial_value, "batch")
        with_totals = sweep == 0
        row_scale_blocks = col_scale.reshape(count, block_cols)
        lines = 2 if with_totals else 1

        def add(running, pair):
            block, scale = pair
            scores = scores_of(views, block)
            found = jnp.sum(jnp.exp(scores / code_temp) * scale[None, :], axis=1)
            if with_totals:
                found = jnp.stack([found, jnp.sum(jnp.exp(scores / pred_temp), axis=1)])
            else:
                found = found[None, :]
            return (running + found, None)

        partial_value, _ = lax.scan(
            add, jnp.zeros((lines, rows), jnp.float32), (unit_blocks, row_scale_blocks)
        )
        summed = of_everyone(partial_value, "proto")
        row_scale = 1.0 / summed[0]
        if sweep == 0:
            totals = summed[1]
    mate_scale = row_scale[pairing]
    scale_blocks = col_scale.reshape(count, block_cols)

    def finish(running, pair):
        block, scale = pair
        scores = scores_of(views, block)
        mate_scores = scores_of(mates, block)
        predicted = jnp.exp(scores / pred_temp) / totals[:, None]
        codes = mate_scale[:, None] * jnp.exp(mate_scores / code_temp) * scale[None, :]
        d_scores = ((predicted - codes) * (loss_scale / pred_temp)).astype(jnp.bfloat16)
        running = running + jnp.dot(d_scores, block, preferred_element_type=jnp.float32)
        unit_part = lax.dot_general(
            d_scores, views, (((0,), (0,)), ((), ())), preferred_element_type=jnp.float32
        )
        return (running, unit_part)

    view_partial, unit_parts = lax.scan(
        finish, jnp.zeros((rows, depth), jnp.float32), (unit_blocks, scale_blocks)
    )
    view_grad = total_of_pieces(view_partial, "proto")
    unit_grad = unit_parts.reshape(width, depth)
    along = jnp.sum(proto_f * unit_grad, axis=1, keepdims=True)
    proto_part = proto_inv * unit_grad - proto_f * (proto_inv * proto_inv * proto_inv) * along
    grad_in, grad_out = head_backward(
        embeddings, w_out, pre_act, hidden, raw_out, inv_norm, view_grad
    )
    grad_proto, grad_in, grad_out = lax.psum((proto_part, grad_in, grad_out), "batch")
    return (grad_in, grad_out, grad_proto)


def solution(mesh):
    return jax.shard_map(
        body,
        mesh=mesh,
        in_specs=(P("batch", None), P("batch"), P(), P(), P("proto", None)),
        out_specs=(P(), P(), P("proto", None)),
        check_vma=False,
    )
```

profile of v0, /device:TPU:0, one launch (start us, length us, event | category | flops | bytes accessed | tf_op | source)
XLA Modules:
  0.0 345.0 jit_solution(7564477604616031568)
XLA Ops:
  8.8 4.1 %multiply_convert_fusion.1 = (bf16[1024,512]{1,0:T(8,128)(2,1)S(1)}, f32[1024,512]{1,0:T(8,128)}) fusion(bf16[1024,1024]{1,0:T(8,128)(2,1)S(1)} %copy-done, bf16[1024,512]{1,0:T(8,128)(2,1)} %param.21), kind=kOutput, calls=%fused_computation.70 | convolution fusion | flops 1078460416 | bytes 6291456 | tf_op jit(solution)/shard_map/dot_general | solution.py:30
  18.8 7.1 %while.82 = (s32[]{:T(128)}, f32[4,1024]{1,0:T(4,128)S(1)}, bf16[4,1024,128]{2,1,0:T(8,128)(2,1)}, bf16[1024,128]{1,0:T(8,128)(2,1)S(1)}, s32[]{:T(128)}, /*index=5*/s32[]{:T(128)}) while((s32[]{:T(128)}, f32[4,1024]{1,0:T(4,128)S(1)}, bf16[4,1024,128]{2,1,0:T(8,128)(2,1)}, bf16[1024,128]{1,0:T(8,128)(2,1)S(1)}, s32[]{:T(128)}, ...), condition=%wide.region_4.5_spmd, body=%wide.region_2.4_spmd.sunk | while | flops 270531584 | bytes 537161 | solution.py:88
  26.8 8.2 %all-to-all-start = ((f32[16,1,4096]{2,1,0:T(1,128)}), f32[16,1,4096]{2,1,0:T(1,128)S(1)}, u32[]{:S(2)}, u32[]{:S(2)}) async-start(f32[16,1,4096]{2,1,0:T(1,128)} %broadcast_in_dim.72), calls=%async_computation | async-start | bytes 524288 | tf_op jit(solution)/shard_map/all_to_all | solution.py:17
  35.0 8.5 %all-to-all-done = f32[16,1,4096]{2,1,0:T(1,128)S(1)} async-done(((f32[16,1,4096]{2,1,0:T(1,128)}), f32[16,1,4096]{2,1,0:T(1,128)S(1)}, u32[]{:S(2)}, u32[]{:S(2)}) %all-to-all-start) | async-done | bytes 262176 | tf_op jit(solution)/shard_map/all_to_all | solution.py:17
  43.7 9.7 %while.85 = (s32[]{:T(128)}, f32[2,1024]{1,0:T(2,128)S(1)}, bf16[4,1024,128]{2,1,0:T(8,128)(2,1)}, bf16[1024,128]{1,0:T(8,128)(2,1)S(1)}, f32[4,1024]{1,0:T(4,128)S(1)}, /*index=5*/s32[]{:T(128)}, s32[]{:T(128)}) while((s32[]{:T(128)}, f32[2,1024]{1,0:T(2,128)S(1)}, bf16[4,1024,128]{2,1,0:T(8,128)(2,1)}, ...), condition=%wide.region_9.10_spmd.clone, body=%wide.region_6.9_spmd.clone.sunk | while | flops 273682432 | bytes 569947 | solution.py:104
  43.7 2.4 multiply_reduce_fusion.14
  46.1 2.4 multiply_reduce_fusion.14
  48.6 2.4 multiply_reduce_fusion.14
  51.0 2.4 multiply_reduce_fusion.14
  54.1 4.3 %all-to-all-start.1 = ((f32[8,2,1024]{2,1,0:T(2,128)}), f32[8,2,1024]{2,1,0:T(2,128)S(1)}, u32[]{:S(2)}, u32[]{:S(2)}) async-start(f32[8,2,1024]{2,1,0:T(2,128)} %broadcast_in_dim.73), calls=%async_computation.1 | async-start | bytes 131072 | tf_op jit(solution)/shard_map/all_to_all | solution.py:17
  58.4 5.6 %all-to-all-done.1 = f32[8,2,1024]{2,1,0:T(2,128)S(1)} async-done(((f32[8,2,1024]{2,1,0:T(2,128)}), f32[8,2,1024]{2,1,0:T(2,128)S(1)}, u32[]{:S(2)}, u32[]{:S(2)}) %all-to-all-start.1) | async-done | bytes 65568 | tf_op jit(solution)/shard_map/all_to_all | solution.py:17
  64.1 7.7 %while.83 = (s32[]{:T(128)}, f32[4,1024]{1,0:T(4,128)S(1)}, f32[1024]{0:T(1024)S(1)}, bf16[4,1024,128]{2,1,0:T(8,128)(2,1)}, bf16[1024,128]{1,0:T(8,128)(2,1)S(1)}, /*index=5*/s32[]{:T(128)}, s32[]{:T(128)}) while((s32[]{:T(128)}, f32[4,1024]{1,0:T(4,128)S(1)}, f32[1024]{0:T(1024)S(1)}, bf16[4,1024,128]{2,1,0:T(8,128)(2,1)}, ...), condition=%wide.region_13.14_spmd, body=%wide.region_11.13_spmd.sunk | while | flops 271580160 | bytes 541265 | solution.py:88
  67.9 1.8 multiply_reduce_fusion.12
  69.8 1.8 multiply_reduce_fusion.12
  72.7 3.6 %all-to-all-start.2 = ((f32[16,1,4096]{2,1,0:T(1,128)}), f32[16,1,4096]{2,1,0:T(1,128)S(1)}, u32[]{:S(2)}, u32[]{:S(2)}) async-start(f32[16,1,4096]{2,1,0:T(1,128)} %broadcast_in_dim.75), calls=%async_computation.2 | async-start | bytes 524288 | tf_op jit(solution)/shard_map/all_to_all | solution.py:17
  76.3 8.5 %all-to-all-done.2 = f32[16,1,4096]{2,1,0:T(1,128)S(1)} async-done(((f32[16,1,4096]{2,1,0:T(1,128)}), f32[16,1,4096]{2,1,0:T(1,128)S(1)}, u32[]{:S(2)}, u32[]{:S(2)}) %all-to-all-start.2) | async-done | bytes 262176 | tf_op jit(solution)/shard_map/all_to_all | solution.py:17
  85.0 7.5 %while.86 = (s32[]{:T(128)}, f32[1,1024]{1,0:T(1,128)S(1)}, bf16[4,1024,128]{2,1,0:T(8,128)(2,1)}, bf16[1024,128]{1,0:T(8,128)(2,1)S(1)}, f32[4,1024]{1,0:T(4,128)S(1)}, /*index=5*/s32[]{:T(128)}, s32[]{:T(128)}) while((s32[]{:T(128)}, f32[1,1024]{1,0:T(1,128)S(1)}, bf16[4,1024,128]{2,1,0:T(8,128)(2,1)}, ...), condition=%wide.region_17.18_spmd.clone, body=%wide.region_15.17_spmd.clone.sunk | while | flops 271582208 | bytes 553563 | solution.py:104
  85.1 1.8 multiply_reduce_fusion.15
  86.9 1.8 multiply_reduce_fusion.15
  88.8 1.8 multiply_reduce_fusion.15
  90.7 1.8 multiply_reduce_fusion.15
  93.2 3.3 all-to-all-start.3
  96.6 5.4 %all-to-all-done.3 = f32[8,1,1024]{2,1,0:T(1,128)S(1)} async-done(((f32[8,1,1024]{2,1,0:T(1,128)}), f32[8,1,1024]{2,1,0:T(1,128)S(1)}, u32[]{:S(2)}, u32[]{:S(2)}) %all-to-all-start.3) | async-done | bytes 32800 | tf_op jit(solution)/shard_map/all_to_all | solution.py:17
  102.0 7.7 %while.84 = (s32[]{:T(128)}, f32[4,1024]{1,0:T(4,128)S(1)}, f32[1024]{0:T(1024)S(1)}, bf16[4,1024,128]{2,1,0:T(8,128)(2,1)}, bf16[1024,128]{1,0:T(8,128)(2,1)S(1)}, /*index=5*/s32[]{:T(128)}, s32[]{:T(128)}) while((s32[]{:T(128)}, f32[4,1024]{1,0:T(4,128)S(1)}, f32[1024]{0:T(1024)S(1)}, bf16[4,1024,128]{2,1,0:T(8,128)(2,1)}, ...), condition=%wide.region_21.22_spmd, body=%wide.region_19.21_spmd.sunk | while | flops 271580160 | bytes 541265 | solution.py:88
  110.6 3.6 %all-to-all-start.4 = ((f32[16,1,4096]{2,1,0:T(1,128)}), f32[16,1,4096]{2,1,0:T(1,128)S(1)}, u32[]{:S(2)}, u32[]{:S(2)}) async-start(f32[16,1,4096]{2,1,0:T(1,128)} %broadcast_in_dim.78), calls=%async_computation.4 | async-start | bytes 524288 | tf_op jit(solution)/shard_map/all_to_all | solution.py:17
  114.2 8.6 %all-to-all-done.4 = f32[16,1,4096]{2,1,0:T(1,128)S(1)} async-done(((f32[16,1,4096]{2,1,0:T(1,128)}), f32[16,1,4096]{2,1,0:T(1,128)S(1)}, u32[]{:S(2)}, u32[]{:S(2)}) %all-to-all-start.4) | async-done | bytes 262176 | tf_op jit(solution)/shard_map/all_to_all | solution.py:17
  123.0 7.5 %while.87 = (s32[]{:T(128)}, f32[1,1024]{1,0:T(1,128)S(1)}, bf16[4,1024,128]{2,1,0:T(8,128)(2,1)}, bf16[1024,128]{1,0:T(8,128)(2,1)S(1)}, f32[4,1024]{1,0:T(4,128)S(1)}, /*index=5*/s32[]{:T(128)}, s32[]{:T(128)}) while((s32[]{:T(128)}, f32[1,1024]{1,0:T(1,128)S(1)}, bf16[4,1024,128]{2,1,0:T(8,128)(2,1)}, ...), condition=%wide.region_25.26_spmd.clone, body=%wide.region_23.25_spmd.clone.sunk | while | flops 271582208 | bytes 553563 | solution.py:104
  131.2 3.3 all-to-all-start.5
  134.8 3.2 gather_fusion.1
  138.0 1.9 all-to-all-done.5
  139.9 4.5 %gather_fusion = f32[1024]{0:T(1024)S(1)} fusion(f32[1024]{0:T(1024)S(1)} %broadcast_divide_fusion.3, s32[1024]{0:T(1024)S(1)} %fusion.51), kind=kCustom, calls=%fused_computation | custom fusion | bytes 12288 | tf_op jit(solution)/shard_map/gather | solution.py:111
  144.5 38.7 %while.88 = (s32[]{:T(128)}, f32[1024,128]{1,0:T(8,128)S(1)}, f32[4,1024,128]{2,1,0:T(8,128)}, bf16[4,1024,128]{2,1,0:T(8,128)(2,1)}, bf16[1024,128]{1,0:T(8,128...) while((s32[]{:T(128)}, f32[1024,128]{1,0:T(8,128)S(1)}, ...), condition=%wide.region_28.29_spmd.clone, body=%wide.region_27.28_spmd.clone.sunk | while | flops 1082392576 | bytes 26237076 | solution.py:127
  146.2 2.7 multiply_convert_fusion.4
  151.7 2.4 convolution_add_fusion.2
  155.8 2.7 multiply_convert_fusion.4
  161.4 2.4 convolution_add_fusion.2
  165.5 2.7 multiply_convert_fusion.4
  171.1 2.4 convolution_add_fusion.2
  175.2 2.7 multiply_convert_fusion.4
  180.8 2.4 convolution_add_fusion.2
  184.1 2.6 fusion.43
  186.7 4.7 %fusion.42 = f32[4096,128]{1,0:T(8,128)} fusion(bf16[4096,128]{1,0:T(8,128)(2,1)S(1)} %copy-done.4, f32[4,1024,128]{2,1,0:T(8,128)} %get-tuple-element.215, f32[4096]{0:T(1024)S(1)} %fusion.43, f32[4096]{0:T(1024)S(1)} %copy-done.11, f32[4096]{0:T(1024)S(1)} %get-tuple-element.587), kind=kLoop, calls=%fused_computation.67 | loop fusion | flops 2621440 | bytes 5292032 | tf_op jit(solution)/shard_map/sub | solution.py:133
  191.4 21.1 %all-gather.3.cloned.1.call-done = f32[8192,128]{1,0:T(8,128)} async-done(((f32[1024,128]{1,0:T(8,128)}), f32[8192,128]{1,0:T(8,128)}) %all-gather.3.cloned.1.call-update) | async-done | bytes 4194320 | tf_op jit(solution)/shard_map/all_gather | solution.py:26
  212.6 3.3 reduce_sum.170
  219.5 5.5 %convolution_bitcast_fusion.1 = f32[1024,512]{0,1:T(8,128)} fusion(bf16[1024,1024]{1,0:T(8,128)(2,1)S(1)} %copy-done, f32[1024,512]{1,0:T(8,128)} %get-tuple-element.593, bf16[1024,128]{0,1:T(8,128)(2,1)S(1)} %subtract_convert_fusion, bf16[512,128]{1,0:T(8,128)(2,1)S(1)} %copy-done.10), kind=kOutput, calls=%fused_computation.71 | convolution fusion | flops 1218445312 | bytes 6684672 | tf_op jit(solution)/shard_map/dot_general | solution.py:50
  225.0 106.4 %all-reduce.3.cloned.1.call-done = (f32[1024,512]{0,1:T(8,128)}, f32[512,128]{1,0:T(8,128)}, f32[4096,128]{1,0:T(8,128)}) async-done(((f32[1024,512]{0,1:T(8,128)}, f32[512,128]{1,0:T(8,128)}, f32[4096,128]{1,0:T(8,128)}), (f32[1024,512]{0,1:T(8,128)}, f32[512,128]{1,0:T(8,128)}, f32[4096,128]{1,0:T(8,128)})) %all-reduce.3.cloned.1.call-update) | async-done | bytes 4456464 | tf_op jit(solution)/shard_map/psum | solution.py:137
  331.4 2.9 copy.64
  335.1 3.0 copy.142
  (149 shorter events, 62.4 us)
Async XLA Ops:
  7.2 1.6 copy-start
  7.2 5.7 %copy-start.10 = (bf16[512,128]{1,0:T(8,128)(2,1)S(1)}, bf16[512,128]{1,0:T(8,128)(2,1)}, u32[]{:S(2)}) copy-start(bf16[512,128]{1,0:T(8,128)(2,1)} %param.22) | copy-start | bytes 393220
  12.9 1.1 copy-start.7
  12.9 3.2 copy-start.3
  13.4 0.8 copy-start.5
  14.0 2.0 copy-start.12
  26.8 16.7 %all-to-all-start = ((f32[16,1,4096]{2,1,0:T(1,128)}), f32[16,1,4096]{2,1,0:T(1,128)S(1)}, u32[]{:S(2)}, u32[]{:S(2)}) async-start(f32[16,1,4096]{2,1,0:T(1,128)} %broadcast_in_dim.72), calls=%async_computation | async-start | bytes 524288 | tf_op jit(solution)/shard_map/all_to_all | solution.py:17
  54.1 9.9 %all-to-all-start.1 = ((f32[8,2,1024]{2,1,0:T(2,128)}), f32[8,2,1024]{2,1,0:T(2,128)S(1)}, u32[]{:S(2)}, u32[]{:S(2)}) async-start(f32[8,2,1024]{2,1,0:T(2,128)} %broadcast_in_dim.73), calls=%async_computation.1 | async-start | bytes 131072 | tf_op jit(solution)/shard_map/all_to_all | solution.py:17
  72.7 12.2 %all-to-all-start.2 = ((f32[16,1,4096]{2,1,0:T(1,128)}), f32[16,1,4096]{2,1,0:T(1,128)S(1)}, u32[]{:S(2)}, u32[]{:S(2)}) async-start(f32[16,1,4096]{2,1,0:T(1,128)} %broadcast_in_dim.75), calls=%async_computation.2 | async-start | bytes 524288 | tf_op jit(solution)/shard_map/all_to_all | solution.py:17
  93.2 8.7 %all-to-all-start.3 = ((f32[8,1,1024]{2,1,0:T(1,128)}), f32[8,1,1024]{2,1,0:T(1,128)S(1)}, u32[]{:S(2)}, u32[]{:S(2)}) async-start(f32[8,1,1024]{2,1,0:T(1,128)} %broadcast_in_dim.76), calls=%async_computation.3 | async-start | bytes 65536 | tf_op jit(solution)/shard_map/all_to_all | solution.py:17
  110.6 12.2 %all-to-all-start.4 = ((f32[16,1,4096]{2,1,0:T(1,128)}), f32[16,1,4096]{2,1,0:T(1,128)S(1)}, u32[]{:S(2)}, u32[]{:S(2)}) async-start(f32[16,1,4096]{2,1,0:T(1,128)} %broadcast_in_dim.78), calls=%async_computation.4 | async-start | bytes 524288 | tf_op jit(solution)/shard_map/all_to_all | solution.py:17
  123.0 11.7 %copy-start.15 = (s32[1024]{0:T(1024)S(1)}, s32[1024]{0:T(1024)}, u32[]{:S(2)}) copy-start(s32[1024]{0:T(1024)} %param.20) | copy-start | bytes 12292
  131.2 8.7 %all-to-all-start.5 = ((f32[8,1,1024]{2,1,0:T(1,128)}), f32[8,1,1024]{2,1,0:T(1,128)S(1)}, u32[]{:S(2)}, u32[]{:S(2)}) async-start(f32[8,1,1024]{2,1,0:T(1,128)} %broadcast_in_dim.79), calls=%async_computation.5 | async-start | bytes 65536 | tf_op jit(solution)/shard_map/all_to_all | solution.py:17
  134.5 78.0 %all-gather.3.cloned.1.call-start = ((), (), s32[]{:S(2)}) async-start(), calls=%async_computation.6 | async-start | bytes 4718592 | tf_op jit(solution)/shard_map/all_gather | solution.py:26
  148.9 1.4 copy-start.1
  158.5 1.4 copy-start.1
  168.2 1.4 copy-start.1
  177.9 1.4 copy-start.1
  183.2 0.8 copy-start.2
  183.2 3.5 %copy-start.11 = (f32[4096]{0:T(1024)S(1)}, f32[4096]{0:T(1024)}, u32[]{:S(2)}) copy-start(f32[4096]{0:T(1024)} %get-tuple-element.586) | copy-start | bytes 49156
  184.0 2.7 copy-start.4
  184.1 147.4 %all-reduce.3.cloned.1.call-start = ((), (), s32[]{:S(2)}) async-start(), calls=%async_computation.7 | async-start | bytes 8912896 | tf_op jit(solution)/shard_map/psum | solution.py:137
  212.6 4.5 %copy-start.6 = (f32[1024,128]{0,1:T(8,128)S(1)}, f32[1024,128]{0,1:T(8,128)}, u32[]{:S(2)}) copy-start(f32[1024,128]{0,1:T(8,128)} %copy-done.5) | copy-start | bytes 1572868
  215.8 1.4 copy-start.13
  215.8 1.4 copy-start.14
  217.1 1.2 copy-start.8
  331.4 2.9 copy-start.9
Sparse Core Ops, SparseCore 0:
  184.2 28.3 all-gather.2
  225.2 106.2 all-reduce.2
where the time goes:
time: 348 us; the launch traced here: 345 us
  waiting for transfers between devices  166 us (48%)
  matrix products  89.6 us (26%)
  local copies, waits for them, and re-layouts  31.5 us (9%)
  starting transfers between devices  26.7 us (8%)
  other arithmetic  15.8 us (5%)
  between operations  14.5 us (4%)
    psum x1, waiting for transfers between devices, body(): lax.psum((proto_part, grad_in, grad_out), 'batch')  106 us
    dot_general x32, matrix products, scores_of(): lax.dot_general(rows_in, unit, (((1,), (1,)), ((), ())), preferred_elemen...  62.6 us
    all_to_all x6, waiting for transfers between devices, from_everyone(): return lax.all_to_all(copies, axis, split_axis=0, concat_axis=0, tiled=True)  38.5 us
    all_to_all x6, starting transfers between devices, from_everyone(): return lax.all_to_all(copies, axis, split_axis=0, concat_axis=0, tiled=True)  26.4 us
    all_gather x1, waiting for transfers between devices, total_of_pieces(): return lax.all_gather(x, axis).sum(0)  21.1 us
    unnamed x37, local copies, waits for them, and re-layouts  11.4 us
    dot_general x4, matrix products, finish(): jnp.dot(d_scores, block, preferred_element_type=jnp.float32)  9.68 us
  transfers between devices with their start and end apart: 8, of which 8 were waited for; matrix products, arithmetic and copies ran while one was open for 3% of the time, Pallas kernels for 0%

commit v1 on v0

v1 whole, which is shorter than its diff:
```python
import math

import jax
import jax.numpy as jnp
from jax import lax
from jax.experimental import pallas as pl
from jax.experimental.pallas import tpu as pltpu
from jax.sharding import PartitionSpec as P

ITERS = 3
norm_eps = 1e-06
loss_gain = 64.0 / 0.1
half_log2 = 10.0 * math.log2(math.e)
gelu_a = math.sqrt(2.0 / math.pi)
gelu_b = 0.044715

F32, BF16 = jnp.float32, jnp.bfloat16
MESH = pl.DeviceIdType.MESH
NB, NP = 16, 8
R, E, H, Z, W = 1024, 1024, 512, 128, 4096
RC = R // NP
CC = W // NB
WV = W // 128


def dot(a, b):
    return jnp.dot(a, b, preferred_element_type=F32)


def dot_t(a, b):
    return lax.dot_general(a, b, (((1,), (1,)), ((), ())), preferred_element_type=F32)


def dot_tl(a, b):
    return lax.dot_general(a, b, (((0,), (0,)), ((), ())), preferred_element_type=F32)


def iota(shape, dim):
    return lax.broadcasted_iota(jnp.int32, shape, dim)


def onehot(mask):
    return jnp.where(mask, 1.0, 0.0).astype(BF16)


def aligned(i, n):
    return pl.ds(pl.multiple_of(i * n, n), n)


def as_row(x):
    return jnp.concatenate([x[k : k + 1, :] for k in range(x.shape[0])], axis=1)


def kernel(
    emb, pairing, w_in, w_out, proto,
    gin, gout, gproto,
    pre, hidden, raw, perm, perm_t, views, views_t, unit, eh, dsc,
    tot_acc, row_b, tot_b, raw_own, c_ref,
    col_send, col_recv, row_send, row_recv,
    vun, vg_send, vg_recv, vg_own, dr_send, dr_all, d_raw, d_pre,
    ug_send, ug_recv, ug_own, gp_send,
    go_f, go_send, go_recv, goa_send, gi_f, gi_send, gi_recv, gx_send,
    col_sem, row_sem, vg_sem, dr_sem, ug_sem, gp_sem, go_sem, goa_sem, gi_sem, gx_sem, gb_sem, gc_sem,
):
    b = lax.axis_index("batch")
    p = lax.axis_index("proto")
    x, core = p // 2, p % 2

    def batch_peer(k):
        return (lax.rem(b + k, NB), p)

    def batch_source(k):
        return lax.rem(b + NB - k, NB)

    def proto_peer(k):
        return (b, lax.rem(p + k, NP))

    def proto_source(k):
        return lax.rem(p + NP - k, NP)

    def copy(src, dst, sem, k, device):
        return pltpu.make_async_remote_copy(
            src_ref=src, dst_ref=dst, send_sem=sem.at[0, k], recv_sem=sem.at[1, k],
            device_id=device, device_id_type=MESH,
        )

    barrier = pltpu.get_barrier_semaphore()

    @pl.loop(1, NB)
    def _(k):
        pl.semaphore_signal(barrier, inc=1, device_id=batch_peer(k), device_id_type=MESH)

    @pl.loop(1, NP)
    def _(k):
        pl.semaphore_signal(barrier, inc=1, device_id=proto_peer(k), device_id_type=MESH)

    @pl.loop(0, R // 256)
    def _(i):
        rows = aligned(i, 256)
        v = dot(emb[rows, :], w_in[...])
        pre[rows, :] = v
        hid = (0.5 * v * (1.0 + jnp.tanh(gelu_a * (v + gelu_b * (v * v * v))))).astype(BF16)
        hidden[rows, :] = hid
        out = dot(hid, w_out[...])
        raw[rows, :] = out
        inv = lax.rsqrt(jnp.sum(out * out, axis=1, keepdims=True) + norm_eps)
        vun[rows, :] = (out * inv).astype(BF16)

    mate = pairing[...]
    lead = mate > iota((8, 128), 0) * 128 + iota((8, 128), 1)
    lead_f = jnp.where(lead, 1.0, 0.0)
    within = dot(lead_f, jnp.where(iota((128, 128), 0) < iota((128, 128), 1), 1.0, 0.0))
    chunk = dot(lead_f, jnp.ones((128, 128), F32))
    before = [jnp.zeros((1, 128), F32)]
    for k in range(7):
        before.append(before[-1] + chunk[k : k + 1, :])
    rank = within + jnp.concatenate(before, axis=0)
    high = jnp.floor(rank * (1.0 / 32.0))
    low = rank - 32.0 * high
    mate_row = as_row(mate)

    @pl.loop(0, 8)
    def _(i):
        perm[aligned(i, 128), :] = onehot(mate_row == iota((128, R), 0) + i * 128)

    halves = jnp.concatenate([as_row(high), as_row(low), jnp.zeros((14, R), F32)], axis=0).astype(BF16)
    of_mate = dot(halves, perm[...])
    lead_row = as_row(lead_f)
    rank_row = jnp.where(lead_row > 0.5, as_row(rank), 32.0 * of_mate[0:1, :] + of_mate[1:2, :])
    pos = rank_row + 64.0 * jnp.floor(rank_row * (1.0 / 64.0)) + jnp.where(lead_row > 0.5, 0.0, 64.0)
    pos = pos.astype(jnp.int32)

    @pl.loop(0, 8)
    def _(i):
        perm[aligned(i, 128), :] = onehot(pos == iota((128, R), 0) + i * 128)

    views[...] = dot(perm[...], vun[...]).astype(BF16)

    @pl.loop(0, W // 256)
    def _(i):
        rows = aligned(i, 256)
        f = proto[rows, :].astype(F32)
        inv = lax.rsqrt(jnp.sum(f * f, axis=1, keepdims=True) + norm_eps)
        unit[rows, :] = (f * inv).astype(BF16)

    tot_acc[...] = jnp.zeros_like(tot_acc)

    @pl.loop(0, W // 512)
    def _(j):
        cols = aligned(j, 512)
        u = unit[cols, :]

        def some_rows(i, acc):
            rows = aligned(i, 256)
            e = jnp.exp2(dot_t(views[rows, :], u) * half_log2)
            eh[rows, cols] = e
            tot_acc[rows, :] += (e[:, 0:128] + e[:, 128:256]) + (e[:, 256:384] + e[:, 384:512])
            return acc + jnp.sum((e * e).reshape(32, 8, 512), axis=0)

        acc = lax.fori_loop(0, R // 256, some_rows, jnp.zeros((8, 512), F32))
        line = jnp.sum(acc, axis=0, keepdims=True)
        for m in range(4):
            col_send[0, pl.ds(j * 4 + m, 1), :] = line[:, m * 128 : m * 128 + 128]

    pl.semaphore_wait(barrier, NB - 1 + NP - 1)

    def start_columns(it):
        @pl.loop(1, NB)
        def _(k):
            copy(col_send.at[it], col_recv.at[it, k], col_sem.at[it], k, batch_peer(k)).start()

    def finish_columns(it):
        @pl.loop(1, NB)
        def _(k):
            copy(col_send.at[it], col_recv.at[it, k], col_sem.at[it], k, batch_peer(k)).wait_recv()

        total = col_send[it]
        for k in range(1, NB):
            total = total + col_recv[it, k]
        c_ref[...] = 1.0 / total

    def start_rows(slot):
        @pl.loop(1, NP)
        def _(k):
            copy(row_send.at[slot], row_recv.at[slot, k], row_sem.at[slot], k, proto_peer(k)).start()

    def finish_rows(slot):
        @pl.loop(1, NP)
        def _(k):
            copy(row_send.at[slot], row_recv.at[slot, k], row_sem.at[slot], k, proto_peer(k)).wait_recv()

        total = row_send[slot]
        for k in range(1, NP):
            total = total + row_recv[slot, k]
        return 1.0 / total

    def to_lines(src, slot):
        for q in range(8):
            row_send[slot, q : q + 1, :] = jnp.sum(src[q * 128 : q * 128 + 128, :].T, axis=0, keepdims=True)

    def spread(lines, dst):
        for q in range(8):
            dst[q * 128 : q * 128 + 128, :] = jnp.broadcast_to(lines[q : q + 1, :], (128, 128)).T

    def column_sweep(it):
        def some_rows(i, acc):
            rows = aligned(i, 8)
            r = row_b[rows, :]
            out = []
            for j in range(WV):
                e = eh[rows, j * 128 : j * 128 + 128]
                out.append(acc[j] + (e * e) * r)
            return tuple(out)

        acc = lax.fori_loop(0, R // 8, some_rows, tuple(jnp.zeros((8, 128), F32) for _ in range(WV)))
        for j in range(WV):
            col_send[it, j : j + 1, :] = jnp.sum(acc[j], axis=0, keepdims=True)

    def row_sweep():
        c = [jnp.broadcast_to(c_ref[j : j + 1, :], (8, 128)) for j in range(WV)]

        @pl.loop(0, R // 8)
        def _(i):
            rows = aligned(i, 8)
            part = [jnp.zeros((8, 128), F32) for _ in range(4)]
            for j in range(WV):
                e = eh[rows, j * 128 : j * 128 + 128]
                part[j % 4] = part[j % 4] + (e * e) * c[j]
            row_b[rows, :] = (part[0] + part[1]) + (part[2] + part[3])

    start_columns(0)

    to_lines(tot_acc, ITERS)
    start_rows(ITERS)
    views_t[...] = views[...].astype(F32).T.astype(BF16)

    @pl.loop(0, R // 256)
    def _(i):
        rows = aligned(i, 256)
        v = pre[rows, :]
        t = jnp.tanh(gelu_a * (v + gelu_b * (v * v * v)))
        pre[rows, :] = 0.5 * (1.0 + t) + 0.5 * v * (1.0 - t * t) * (gelu_a * (1.0 + 3.0 * gelu_b * (v * v)))

    finish_columns(0)
    row_sweep()
    to_lines(row_b, 0)
    start_rows(0)

    for q in range(8):
        at = jnp.broadcast_to(pos[:, q * 128 : q * 128 + 128], (128, 128)).astype(F32).T
        for k in range(8):
            here = (iota((128, 128), 1) + k * 128).astype(F32)
            perm_t[q * 128 : q * 128 + 128, k * 128 : k * 128 + 128] = onehot(at == here)

    spread(finish_rows(0), row_b)
    column_sweep(1)
    start_columns(1)

    own = perm[aligned(p, RC), :]
    r0 = raw[...]
    r1 = r0.astype(BF16)
    r0 = r0 - r1.astype(F32)
    r2 = r0.astype(BF16)
    r3 = (r0 - r2.astype(F32)).astype(BF16)
    raw_own[...] = dot(own, r1) + dot(own, r2) + dot(own, r3)
    spread(finish_rows(ITERS) * loss_gain, tot_b)

    finish_columns(1)
    row_sweep()
    to_lines(row_b, 1)
    start_rows(1)
    spread(finish_rows(1), row_b)
    column_sweep(2)
    start_columns(2)
    finish_columns(2)
    row_sweep()
    to_lines(row_b, 2)
    start_rows(2)
    spread(finish_rows(2) * loss_gain, row_b)

    def view_copy(k):
        return copy(vg_send.at[k], vg_recv.at[k], vg_sem, k, proto_peer(k))

    @pl.loop(1, NP + 1)
    def _(k):
        q = lax.rem(p + k, NP)
        top, low_half = aligned(2 * q, 64), aligned(2 * q + 1, 64)
        t_top, t_low = tot_b[top, :], tot_b[low_half, :]
        r_top, r_low = row_b[top, :], row_b[low_half, :]

        @pl.loop(0, WV)
        def _(j):
            cols = aligned(j, 128)
            c = c_ref[pl.ds(j, 1), :]
            e_top, e_low = eh[top, cols], eh[low_half, cols]
            dsc[top, cols] = (e_top * t_top - (e_low * e_low) * c * r_low).astype(BF16)
            dsc[low_half, cols] = (e_low * t_low - (e_top * e_top) * c * r_top).astype(BF16)

        part = dot(dsc[aligned(q, RC), :], unit[...])
        vg_send[lax.rem(k, NP)] = part.astype(BF16)

        @pl.when(k < NP)
        def _():
            view_copy(k).start()

        @pl.when(k == NP)
        def _():
            vg_own[...] = part

    def unit_copy(k):
        return copy(ug_send.at[k], ug_recv.at[k], ug_sem, k, batch_peer(k))

    @pl.loop(1, NB + 1)
    def _(k):
        q = lax.rem(b + k, NB)
        part = dot(views_t[...], dsc[:, aligned(q, CC)])

        @pl.when(k < NB)
        def _():
            ug_send[k] = part.astype(BF16)
            unit_copy(k).start()

        @pl.when(k == NB)
        def _():
            ug_own[...] = part

    view_grad = vg_own[...]
    for k in range(1, NP):
        view_copy(k).wait_recv()
        view_grad = view_grad + vg_recv[k].astype(F32)
    out = raw_own[...]
    inv = lax.rsqrt(jnp.sum(out * out, axis=1, keepdims=True) + norm_eps)
    along = jnp.sum(out * view_grad, axis=1, keepdims=True)
    mine = (inv * view_grad - out * (inv * inv * inv) * along).astype(BF16)
    dr_send[...] = mine
    dr_all[aligned(p, RC), :] = mine

    def raw_copy(k, owner):
        return copy(dr_send, dr_all.at[aligned(owner, RC), :], dr_sem, k, proto_peer(k))

    @pl.loop(1, NP)
    def _(k):
        raw_copy(k, p).start()

    @pl.loop(1, NP)
    def _(k):
        raw_copy(k, proto_source(k)).wait_recv()

    d_raw[...] = dot(perm_t[...], dr_all[...]).astype(BF16)

    go = dot_tl(hidden[...], d_raw[...]).reshape(NB, H // NB, Z)
    go_f[...] = go
    go_send[...] = go.astype(BF16)

    def out_copy(k):
        return copy(go_send.at[lax.rem(b + k, NB)], go_recv.at[k], go_sem, k, batch_peer(k))

    @pl.loop(1, NB)
    def _(k):
        out_copy(k).start()

    @pl.loop(0, R // 256)
    def _(i):
        rows = aligned(i, 256)
        d_pre[rows, :] = (pre[rows, :] * dot_t(d_raw[rows, :], w_out[...])).astype(BF16)

    part_of = core * 4 + x
    gi = dot_tl(emb[:, aligned(part_of, 128)], d_pre[...]).reshape(8, 16, H)
    gi_f[...] = gi
    gi_send[...] = gi.astype(BF16)

    def half(q):
        return aligned(q % 2, 256)

    def in_copy(k):
        q = lax.rem(b + k, NB)
        return copy(gi_send.at[q // 2, :, half(q)], gi_recv.at[k], gi_sem, k, batch_peer(k))

    @pl.loop(1, NB)
    def _(k):
        in_copy(k).start()

    @pl.loop(1, NB)
    def _(k):
        in_copy(k).wait_recv()

    total = gi_f[b // 2, :, half(b)]
    for k in range(1, NB):
        total = total + gi_recv[k].astype(F32)
    total = total.astype(BF16)
    gx_send[...] = total
    gin[part_of, b // 2, :, half(b)] = total

    def along_x(k, owner):
        peer = (b, lax.rem(x + k, 4) * 2 + core)
        return copy(gx_send, gin.at[core * 4 + owner, b // 2, :, half(b)], gx_sem, k, peer)

    @pl.loop(1, 4)
    def _(k):
        along_x(k, x).start()

    grad = ug_own[...]
    for k in range(1, NB):
        unit_copy(k).wait_recv()
        grad = grad + ug_recv[k].astype(F32)
    grad = grad.T
    f = proto[aligned(b, CC), :].astype(F32)
    inv = lax.rsqrt(jnp.sum(f * f, axis=1, keepdims=True) + norm_eps)
    along = jnp.sum(f * grad, axis=1, keepdims=True)
    grad = (inv * grad - f * (inv * inv * inv) * along).astype(BF16)
    gp_send[...] = grad
    gproto[aligned(b, CC), :] = grad

    def proto_copy(k, owner):
        return copy(gp_send, gproto.at[aligned(owner, CC), :], gp_sem, k, batch_peer(k))

    @pl.loop(1, NB)
    def _(k):
        proto_copy(k, b).start()

    total = go_f[b]
    for k in range(1, NB):
        out_copy(k).wait_recv()
        total = total + go_recv[k].astype(F32)
    total = total.astype(BF16)
    goa_send[...] = total
    gout[b] = total

    def out_all(k, owner):
        return copy(goa_send, gout.at[owner], goa_sem, k, batch_peer(k))

    @pl.loop(1, NB)
    def _(k):
        out_all(k, b).start()

    @pl.loop(1, 4)
    def _(k):
        along_x(k, lax.rem(x + 4 - k, 4)).wait_recv()

    def plane(q, c):
        return gin.at[pl.ds(c * 4, 4), q // 2, :, half(q)]

    def along_batch(k, owner):
        return copy(plane(owner, core), plane(owner, core), gb_sem, k, batch_peer(k))

    @pl.loop(1, NB)
    def _(k):
        along_batch(k, b).start()

    def to_core(k, c):
        q = batch_source(k)
        return copy(plane(q, c), plane(q, c), gc_sem, k, (b, x * 2 + 1 - core))

    to_core(0, core).start()

    @pl.loop(1, NB)
    def _(k):
        along_batch(k, batch_source(k)).wait_recv()
        to_core(k, core).start()

    @pl.loop(0, NB)
    def _(k):
        to_core(k, 1 - core).wait_recv()
        to_core(k, core).wait_send()

    @pl.loop(1, NB)
    def _(k):
        proto_copy(k, batch_source(k)).wait_recv()
        out_all(k, batch_source(k)).wait_recv()
        for it in range(ITERS):
            copy(col_send.at[it], col_recv.at[it, k], col_sem.at[it], k, batch_peer(k)).wait_send()
        unit_copy(k).wait_send()
        proto_copy(k, b).wait_send()
        out_copy(k).wait_send()
        out_all(k, b).wait_send()
        in_copy(k).wait_send()
        along_batch(k, b).wait_send()

    @pl.loop(1, NP)
    def _(k):
        for slot in range(ITERS + 1):
            copy(row_send.at[slot], row_recv.at[slot, k], row_sem.at[slot], k, proto_peer(k)).wait_send()
        view_copy(k).wait_send()
        raw_copy(k, p).wait_send()

    @pl.loop(1, 4)
    def _(k):
        along_x(k, x).wait_send()


def body(embeddings, pairing, w_in, w_out, prototypes):
    vmem = pl.BlockSpec(memory_space=pltpu.VMEM)
    out = lambda *shape: jax.ShapeDtypeStruct(shape, BF16)
    dma = lambda *shape: pltpu.SemaphoreType.DMA(shape)
    v = pltpu.VMEM
    grad_in, grad_out, grad_proto = pl.pallas_call(
        kernel,
        name="swav_step",
        out_shape=(out(NP, 8, 16, H), out(NB, H // NB, Z), out(W, Z)),
        in_specs=[vmem] * 5,
        out_specs=(vmem,) * 3,
        scratch_shapes=[
            v((R, H), F32), v((R, H), BF16), v((R, Z), F32), v((R, R), BF16), v((R, R), BF16),
            v((R, Z), BF16), v((Z, R), BF16), v((W, Z), BF16), v((R, W), F32), v((R, W), BF16),
            v((R, 128), F32), v((R, 128), F32), v((R, 128), F32), v((RC, Z), F32), v((WV, 128), F32),
            v((ITERS, WV, 128), F32), v((ITERS, NB, WV, 128), F32),
            v((ITERS + 1, 8, 128), F32), v((ITERS + 1, NP, 8, 128), F32),
            v((R, Z), BF16), v((NP, RC, Z), BF16), v((NP, RC, Z), BF16), v((RC, Z), F32),
            v((RC, Z), BF16), v((R, Z), BF16), v((R, Z), BF16), v((R, H), BF16),
            v((NB, Z, CC), BF16), v((NB, Z, CC), BF16), v((Z, CC), F32), v((CC, Z), BF16),
            v((NB, H // NB, Z), F32), v((NB, H // NB, Z), BF16), v((NB, H // NB, Z), BF16), v((H // NB, Z), BF16),
            v((8, 16, H), F32), v((8, 16, H), BF16), v((NB, 16, 256), BF16), v((16, 256), BF16),
            dma(ITERS, 2, NB), dma(ITERS + 1, 2, NP), dma(2, NP), dma(2, NP), dma(2, NB), dma(2, NB),
            dma(2, NB), dma(2, NB), dma(2, NB), dma(2, 4), dma(2, NB), dma(2, NB),
        ],
        compiler_params=pltpu.CompilerParams(
            collective_id=0, has_side_effects=True, vmem_limit_bytes=60 << 20
        ),
    )(embeddings, pairing.reshape(8, 128), w_in, w_out, prototypes)
    return (
        grad_in.reshape(E, H).astype(F32),
        grad_out.reshape(H, Z).astype(F32),
        grad_proto.astype(F32),
    )


def solution(mesh):
    return jax.shard_map(
        body,
        mesh=mesh,
        in_specs=(P("batch", None), P("batch"), P(), P(), P("proto", None)),
        out_specs=(P(), P(), P("proto", None)),
        check_vma=False,
    )
```

time: 348 us -> 135 us (0.39)
  waiting for transfers between devices: 166 us -> 0 us
  Pallas kernels: 0 us -> 128 us
  matrix products: 89.6 us -> 0 us
  local copies, waits for them, and re-layouts: 31.5 us -> 0.01 us
  starting transfers between devices: 26.7 us -> 0 us
  between operations: 14.5 us -> 0.65 us
  other arithmetic: 15.8 us -> 5.11 us
    pallas_call x0 -> x1, Pallas kernels: none -> 128 us  [body(): pl.pallas_call(kernel, name='swav_step', out_shape=(out(NP, 8, 16, H), ou...]
    psum x1 -> x0, waiting for transfers between devices: 106 us -> none  [body(): lax.psum((proto_part, grad_in, grad_out), 'batch')]
    dot_general x44 -> x0, matrix products: 89.6 us -> none  [the longest x32 62.6 us: scores_of(): lax.dot_general(rows_in, unit, (((1,), (1,)), ((), ())), preferred_elemen...]
    all_to_all x6 -> x0, waiting for transfers between devices: 38.5 us -> none  [from_everyone(): return lax.all_to_all(copies, axis, split_axis=0, concat_axis=0, tiled=True)]
    all_to_all x6 -> x0, starting transfers between devices: 26.4 us -> none  [from_everyone(): return lax.all_to_all(copies, axis, split_axis=0, concat_axis=0, tiled=True)]
    all_gather x1 -> x0, waiting for transfers between devices: 21.1 us -> none  [total_of_pieces(): return lax.all_gather(x, axis).sum(0)]
    unnamed x37 -> x4, local copies, waits for them, and re-layouts: 11.4 us -> 0.01 us
    gather x2 -> x0, local copies, waits for them, and re-layouts: 7.74 us -> none  [the longest x1 4.53 us: body(): mate_scale = row_scale[pairing]]
  transfers between devices with their start and end apart: 8 -> 0, of which waited for: 8 -> 0; matrix products, arithmetic and copies ran while one was open for 3% -> 0% of each run, Pallas kernels for 0% -> 0%
where the time goes in v1:
time: 135 us; the launch traced here: 134 us
  Pallas kernels  128 us (95%)
  other arithmetic  5.11 us (4%)
    pallas_call x1, Pallas kernels, body(): pl.pallas_call(kernel, name='swav_step', out_shape=(out(NP, 8, 16, H), ou...  128 us
    convert_element_type x1, other arithmetic, body(): grad_in.reshape(E, H).astype(F32)  2.92 us

profile of v1, /device:TPU:0, one launch (start us, length us, event | category | flops | bytes accessed | tf_op | source)
XLA Modules:
  0.0 133.7 jit_solution(592099382185931793)
XLA Ops:
  0.6 127.9 %swav_step.1 = (bf16[8,8,16,512]{3,2,1,0:T(8,128)(2,1)}, bf16[16,32,128]{2,1,0:T(8,128)(2,1)}, bf16[4096,128]{1,0:T(8,128)(2,1)}) custom-call(bf16[1024,1024]{1,0:T(8,128)(2,1)} %emb.1, s32[8,128]{1,0:T(8,128)} %bitcast.7, bf16[1024,512]{1,0:T(8,128)(2,1)} %w_in.1, bf16[512,128]{1,0:T(8,128)(2,1)} %w_out.1, bf16[4096,128]{1,0:T(8,128)(2,1)} %proto.1), custom_call_target="tpu_custom_call" | custom-call | tf_op jit(solution)/shard_map/swav_step/pallas_call | solution.py:496
  128.5 0.0 copy-start
  128.6 2.9 %bitcast_convert_fusion = f32[1024,512]{1,0:T(8,128)} fusion(bf16[8,8,16,512]{3,2,1,0:T(8,128)(2,1)} %get-tuple-element.6), kind=kLoop, calls=%fused_computation | loop fusion | flops 524288 | bytes 3145728 | tf_op jit(solution)/shard_map/convert_element_type | solution.py:521
  131.5 0.0 copy-start.1
  131.5 0.0 copy-done
  131.5 1.5 %convert_element_type.19 = f32[4096,128]{1,0:T(8,128)} convert(bf16[4096,128]{1,0:T(8,128)(2,1)S(1)} %copy-done) | non-fusion elementwise | flops 524288 | bytes 3145728 | tf_op jit(solution)/shard_map/convert_element_type | solution.py:523
  132.9 0.0 copy-done.1
  132.9 0.7 bitcast_convert_fusion.1
Async XLA Ops:
  128.5 2.9 %copy-start = (bf16[4096,128]{1,0:T(8,128)(2,1)S(1)}, bf16[4096,128]{1,0:T(8,128)(2,1)}, u32[]{:S(2)}) copy-start(bf16[4096,128]{1,0:T(8,128)(2,1)} %get-tuple-element.8) | copy-start | bytes 3145732
  131.5 1.5 %copy-start.1 = (bf16[16,32,128]{2,1,0:T(8,128)(2,1)S(1)}, bf16[16,32,128]{2,1,0:T(8,128)(2,1)}, u32[]{:S(2)}) copy-start(bf16[16,32,128]{2,1,0:T(8,128)(2,1)} %get-tuple-element.7) | copy-start | bytes 393220

commit v2 on v1

--- a/solution.py
+++ b/solution.py
@@ -56,7 +56,7 @@
     gin, gout, gproto,
     pre, hidden, raw, perm, perm_t, views, views_t, unit, eh, dsc,
     tot_acc, row_b, tot_b, raw_own, c_ref,
-    col_send, col_recv, row_send, row_recv,
+    col_line, col_send, col_recv, row_send, row_recv,
     vun, vg_send, vg_recv, vg_own, dr_send, dr_all, d_raw, d_pre,
     ug_send, ug_recv, ug_own, gp_send,
     go_f, go_send, go_recv, goa_send, gi_f, gi_send, gi_recv, gx_send,
@@ -151,20 +151,22 @@
         u = unit[cols, :]
 
         def some_rows(i, acc):
-            rows = aligned(i, 256)
+            rows = aligned(i, 128)
             e = jnp.exp2(dot_t(views[rows, :], u) * half_log2)
             eh[rows, cols] = e
             tot_acc[rows, :] += (e[:, 0:128] + e[:, 128:256]) + (e[:, 256:384] + e[:, 384:512])
-            return acc + jnp.sum((e * e).reshape(32, 8, 512), axis=0)
-
-        acc = lax.fori_loop(0, R // 256, some_rows, jnp.zeros((8, 512), F32))
+            return acc + jnp.sum((e * e).reshape(16, 8, 512), axis=0)
+
+        acc = lax.fori_loop(0, R // 128, some_rows, jnp.zeros((8, 512), F32), unroll=8)
         line = jnp.sum(acc, axis=0, keepdims=True)
         for m in range(4):
-            col_send[0, pl.ds(j * 4 + m, 1), :] = line[:, m * 128 : m * 128 + 128]
+            col_line[pl.ds(j * 4 + m, 1), :] = line[:, m * 128 : m * 128 + 128]
 
     pl.semaphore_wait(barrier, NB - 1 + NP - 1)
 
     def start_columns(it):
+        col_send[it] = col_line[...].astype(BF16)
+
         @pl.loop(1, NB)
         def _(k):
             copy(col_send.at[it], col_recv.at[it, k], col_sem.at[it], k, batch_peer(k)).start()
@@ -174,9 +176,9 @@
         def _(k):
             copy(col_send.at[it], col_recv.at[it, k], col_sem.at[it], k, batch_peer(k)).wait_recv()
 
-        total = col_send[it]
+        total = col_send[it].astype(F32)
         for k in range(1, NB):
-            total = total + col_recv[it, k]
+            total = total + col_recv[it, k].astype(F32)
         c_ref[...] = 1.0 / total
 
     def start_rows(slot):
@@ -202,7 +204,7 @@
         for q in range(8):
             dst[q * 128 : q * 128 + 128, :] = jnp.broadcast_to(lines[q : q + 1, :], (128, 128)).T
 
-    def column_sweep(it):
+    def column_sweep():
         def some_rows(i, acc):
             rows = aligned(i, 8)
             r = row_b[rows, :]
@@ -214,7 +216,7 @@
 
         acc = lax.fori_loop(0, R // 8, some_rows, tuple(jnp.zeros((8, 128), F32) for _ in range(WV)))
         for j in range(WV):
-            col_send[it, j : j + 1, :] = jnp.sum(acc[j], axis=0, keepdims=True)
+            col_line[j : j + 1, :] = jnp.sum(acc[j], axis=0, keepdims=True)
 
     def row_sweep():
         c = [jnp.broadcast_to(c_ref[j : j + 1, :], (8, 128)) for j in range(WV)]
@@ -253,7 +255,7 @@
             perm_t[q * 128 : q * 128 + 128, k * 128 : k * 128 + 128] = onehot(at == here)
 
     spread(finish_rows(0), row_b)
-    column_sweep(1)
+    column_sweep()
     start_columns(1)
 
     own = perm[aligned(p, RC), :]
@@ -270,7 +272,7 @@
     to_lines(row_b, 1)
     start_rows(1)
     spread(finish_rows(1), row_b)
-    column_sweep(2)
+    column_sweep()
     start_columns(2)
     finish_columns(2)
     row_sweep()
@@ -284,17 +286,18 @@
     @pl.loop(1, NP + 1)
     def _(k):
         q = lax.rem(p + k, NP)
-        top, low_half = aligned(2 * q, 64), aligned(2 * q + 1, 64)
-        t_top, t_low = tot_b[top, :], tot_b[low_half, :]
-        r_top, r_low = row_b[top, :], row_b[low_half, :]
-
-        @pl.loop(0, WV)
-        def _(j):
-            cols = aligned(j, 128)
-            c = c_ref[pl.ds(j, 1), :]
-            e_top, e_low = eh[top, cols], eh[low_half, cols]
-            dsc[top, cols] = (e_top * t_top - (e_low * e_low) * c * r_low).astype(BF16)
-            dsc[low_half, cols] = (e_low * t_low - (e_top * e_top) * c * r_top).astype(BF16)
+
+        @pl.loop(0, 4)
+        def _(h):
+            top, low = aligned(q * 8 + h, 16), aligned(q * 8 + h + 4, 16)
+            t_top, t_low = tot_b[top, :], tot_b[low, :]
+            r_top, r_low = row_b[top, :], row_b[low, :]
+            for j in range(WV):
+                cols = slice(j * 128, j * 128 + 128)
+                c = c_ref[j : j + 1, :]
+                e_top, e_low = eh[top, cols], eh[low, cols]
+                dsc[top, cols] = (e_top * t_top - (e_low * e_low) * c * r_low).astype(BF16)
+                dsc[low, cols] = (e_low * t_low - (e_top * e_top) * c * r_top).astype(BF16)
 
         part = dot(dsc[aligned(q, RC), :], unit[...])
         vg_send[lax.rem(k, NP)] = part.astype(BF16)
@@ -348,17 +351,6 @@
 
     d_raw[...] = dot(perm_t[...], dr_all[...]).astype(BF16)
 
-    go = dot_tl(hidden[...], d_raw[...]).reshape(NB, H // NB, Z)
-    go_f[...] = go
-    go_send[...] = go.astype(BF16)
-
-    def out_copy(k):
-        return copy(go_send.at[lax.rem(b + k, NB)], go_recv.at[k], go_sem, k, batch_peer(k))
-
-    @pl.loop(1, NB)
-    def _(k):
-        out_copy(k).start()
-
     @pl.loop(0, R // 256)
     def _(i):
         rows = aligned(i, 256)
@@ -379,25 +371,6 @@
     @pl.loop(1, NB)
     def _(k):
         in_copy(k).start()
-
-    @pl.loop(1, NB)
-    def _(k):
-        in_copy(k).wait_recv()
-
-    total = gi_f[b // 2, :, half(b)]
-    for k in range(1, NB):
-        total = total + gi_recv[k].astype(F32)
-    total = total.astype(BF16)
-    gx_send[...] = total
-    gin[part_of, b // 2, :, half(b)] = total
-
-    def along_x(k, owner):
-        peer = (b, lax.rem(x + k, 4) * 2 + core)
-        return copy(gx_send, gin.at[core * 4 + owner, b // 2, :, half(b)], gx_sem, k, peer)
-
-    @pl.loop(1, 4)
-    def _(k):
-        along_x(k, x).start()
 
     grad = ug_own[...]
     for k in range(1, NB):
@@ -414,9 +387,39 @@
     def proto_copy(k, owner):
         return copy(gp_send, gproto.at[aligned(owner, CC), :], gp_sem, k, batch_peer(k))
 
-    @pl.loop(1, NB)
+    @pl.loop(1, NB // 2)
     def _(k):
         proto_copy(k, b).start()
+
+    go = dot_tl(hidden[...], d_raw[...]).reshape(NB, H // NB, Z)
+    go_f[...] = go
+    go_send[...] = go.astype(BF16)
+
+    def out_copy(k):
+        return copy(go_send.at[lax.rem(b + k, NB)], go_recv.at[k], go_sem, k, batch_peer(k))
+
+    @pl.loop(1, NB)
+    def _(k):
+        out_copy(k).start()
+
+    @pl.loop(1, NB)
+    def _(k):
+        in_copy(k).wait_recv()
+
+    total = gi_f[b // 2, :, half(b)]
+    for k in range(1, NB):
+        total = total + gi_recv[k].astype(F32)
+    total = total.astype(BF16)
+    gx_send[...] = total
+    gin[part_of, b // 2, :, half(b)] = total
+
+    def along_x(k, owner):
+        peer = (b, lax.rem(x + k, 4) * 2 + core)
+        return copy(gx_send, gin.at[core * 4 + owner, b // 2, :, half(b)], gx_sem, k, peer)
+
+    @pl.loop(1, 4)
+    def _(k):
+        along_x(k, x).start()
 
     total = go_f[b]
     for k in range(1, NB):
@@ -446,6 +449,10 @@
     @pl.loop(1, NB)
     def _(k):
         along_batch(k, b).start()
+
+    @pl.loop(NB // 2, NB)
+    def _(k):
+        proto_copy(k, b).start()
 
     def to_core(k, c):
         q = batch_source(k)
@@ -503,7 +510,7 @@
             v((R, H), F32), v((R, H), BF16), v((R, Z), F32), v((R, R), BF16), v((R, R), BF16),
             v((R, Z), BF16), v((Z, R), BF16), v((W, Z), BF16), v((R, W), F32), v((R, W), BF16),
             v((R, 128), F32), v((R, 128), F32), v((R, 128), F32), v((RC, Z), F32), v((WV, 128), F32),
-            v((ITERS, WV, 128), F32), v((ITERS, NB, WV, 128), F32),
+            v((WV, 128), F32), v((ITERS, WV, 128), BF16), v((ITERS, NB, WV, 128), BF16),
             v((ITERS + 1, 8, 128), F32), v((ITERS + 1, NP, 8, 128), F32),
             v((R, Z), BF16), v((NP, RC, Z), BF16), v((NP, RC, Z), BF16), v((RC, Z), F32),
             v((RC, Z), BF16), v((R, Z), BF16), v((R, Z), BF16), v((R, H), BF16),

time: 135 us -> 126 us (0.933)
  Pallas kernels: 128 us -> 120 us
    pallas_call x1, Pallas kernels: 128 us -> 120 us  [body(): pl.pallas_call(kernel, name='swav_step', out_shape=(out(NP, 8, 16, H), ou...]
where the time goes in v2:
time: 126 us
  Pallas kernels  120 us (95%)
  other arithmetic  5.11 us (4%)
    pallas_call x1, Pallas kernels, body(): pl.pallas_call(kernel, name='swav_step', out_shape=(out(NP, 8, 16, H), ou...  120 us
    convert_element_type x1, other arithmetic, body(): grad_in.reshape(E, H).astype(F32)  2.92 us

profile of v2, /device:TPU:0, one launch (start us, length us, event | category | flops | bytes accessed | tf_op | source)
XLA Modules:
  0.0 126.0 jit_solution(8132877312693096743)
XLA Ops:
  0.6 120.2 %swav_step.1 = (bf16[8,8,16,512]{3,2,1,0:T(8,128)(2,1)}, bf16[16,32,128]{2,1,0:T(8,128)(2,1)}, bf16[4096,128]{1,0:T(8,128)(2,1)}) custom-call(bf16[1024,1024]{1,0:T(8,128)(2,1)} %emb.1, s32[8,128]{1,0:T(8,128)} %bitcast.7, bf16[1024,512]{1,0:T(8,128)(2,1)} %w_in.1, bf16[512,128]{1,0:T(8,128)(2,1)} %w_out.1, bf16[4096,128]{1,0:T(8,128)(2,1)} %proto.1), custom_call_target="tpu_custom_call" | custom-call | tf_op jit(solution)/shard_map/swav_step/pallas_call | solution.py:503
  120.8 0.0 copy-start
  120.9 2.9 %bitcast_convert_fusion = f32[1024,512]{1,0:T(8,128)} fusion(bf16[8,8,16,512]{3,2,1,0:T(8,128)(2,1)} %get-tuple-element.6), kind=kLoop, calls=%fused_computation | loop fusion | flops 524288 | bytes 3145728 | tf_op jit(solution)/shard_map/convert_element_type | solution.py:528
  123.8 0.0 copy-start.1
  123.8 0.0 copy-done
  123.8 1.5 %convert_element_type.19 = f32[4096,128]{1,0:T(8,128)} convert(bf16[4096,128]{1,0:T(8,128)(2,1)S(1)} %copy-done) | non-fusion elementwise | flops 524288 | bytes 3145728 | tf_op jit(solution)/shard_map/convert_element_type | solution.py:530
  125.2 0.0 copy-done.1
  125.2 0.7 bitcast_convert_fusion.1
Async XLA Ops:
  120.8 2.9 %copy-start = (bf16[4096,128]{1,0:T(8,128)(2,1)S(1)}, bf16[4096,128]{1,0:T(8,128)(2,1)}, u32[]{:S(2)}) copy-start(bf16[4096,128]{1,0:T(8,128)(2,1)} %get-tuple-element.8) | copy-start | bytes 3145732
  123.8 1.5 %copy-start.1 = (bf16[16,32,128]{2,1,0:T(8,128)(2,1)S(1)}, bf16[16,32,128]{2,1,0:T(8,128)(2,1)}, u32[]{:S(2)}) copy-start(bf16[16,32,128]{2,1,0:T(8,128)(2,1)} %get-tuple-element.7) | copy-start | bytes 393220

commit v3 on v2

--- a/solution.py
+++ b/solution.py
@@ -58,13 +58,14 @@
     tot_acc, row_b, tot_b, raw_own, c_ref,
     col_line, col_send, col_recv, row_send, row_recv,
     vun, vg_send, vg_recv, vg_own, dr_send, dr_all, d_raw, d_pre,
-    ug_send, ug_recv, ug_own, gp_send,
+    ua_send, ua_recv, ua_own, ub_send, ub_recv, ub_own, sa_send, sa_recv, sb_send, sb_recv,
     go_f, go_send, go_recv, goa_send, gi_f, gi_send, gi_recv, gx_send,
-    col_sem, row_sem, vg_sem, dr_sem, ug_sem, gp_sem, go_sem, goa_sem, gi_sem, gx_sem, gb_sem, gc_sem,
+    col_sem, row_sem, vg_sem, dr_sem, up_sem, go_sem, goa_sem, gi_sem, ax_sem, ab_sem, ac_sem, bb_sem, bx_sem, bc_sem,
 ):
     b = lax.axis_index("batch")
     p = lax.axis_index("proto")
     x, core = p // 2, p % 2
+    y, z = b // 4, b % 4
 
     def batch_peer(k):
         return (lax.rem(b + k, NB), p)
@@ -310,22 +311,48 @@
         def _():
             vg_own[...] = part
 
-    def unit_copy(k):
-        return copy(ug_send.at[k], ug_recv.at[k], ug_sem, k, batch_peer(k))
-
-    @pl.loop(1, NB + 1)
-    def _(k):
-        q = lax.rem(b + k, NB)
-        part = dot(views_t[...], dsc[:, aligned(q, CC)])
-
-        @pl.when(k < NB)
+    def y_peer(k):
+        return (lax.rem(y + k, 4) * 4 + z, p)
+
+    def z_peer(k):
+        return (y * 4 + lax.rem(z + k, 4), p)
+
+    def back(i, k):
+        return lax.rem(i + 4 - k, 4)
+
+    def first_a(k):
+        return copy(ua_send.at[k], ua_recv.at[k], up_sem.at[0], k, y_peer(k))
+
+    def first_b(k):
+        return copy(ub_send.at[k], ub_recv.at[k], up_sem.at[1], k, z_peer(k))
+
+    @pl.loop(1, 5)
+    def _(kk):
+        k = lax.rem(kk, 4)
+        to_y = lax.rem(y + k, 4)
+
+        @pl.loop(0, 4)
+        def _(m):
+            to_z = lax.rem(z + m, 4)
+            part = dot(views_t[...], dsc[:, aligned(to_y * 4 + to_z, CC)])
+            ua_send[k, to_z] = part[:, :Z].astype(BF16)
+            ub_send[m, to_y] = part[:, Z:].astype(BF16)
+
+            @pl.when(k == 0)
+            def _():
+                ua_own[to_z] = part[:, :Z]
+
+            @pl.when(m == 0)
+            def _():
+                ub_own[to_y] = part[:, Z:]
+
+        @pl.when(kk < 4)
         def _():
-            ug_send[k] = part.astype(BF16)
-            unit_copy(k).start()
-
-        @pl.when(k == NB)
-        def _():
-            ug_own[...] = part
+            first_a(kk).start()
+
+    @pl.loop(1, 4)
+    def _(k):
+        first_b(k).start()
 
     view_grad = vg_own[...]
     for k in range(1, NP):
@@ -358,38 +385,45 @@
 
     part_of = core * 4 + x
     gi = dot_tl(emb[:, aligned(part_of, 128)], d_pre[...]).reshape(8, 16, H)
-    gi_f[...] = gi
-    gi_send[...] = gi.astype(BF16)
-
-    def half(q):
-        return aligned(q % 2, 256)
+    for m in range(2):
+        gi_m = jnp.concatenate([gi[:, :, m * 128 : m * 128 + 128], gi[:, :, m * 128 + 256 : m * 128 + 384]], axis=2)
+        gi_f[:, m] = gi_m
+        gi_send[:, m] = gi_m.astype(BF16)
 
     def in_copy(k):
         q = lax.rem(b + k, NB)
-        return copy(gi_send.at[q // 2, :, half(q)], gi_recv.at[k], gi_sem, k, batch_peer(k))
+        return copy(gi_send.at[q // 2, q % 2], gi_recv.at[k], gi_sem, k, batch_peer(k))
 
     @pl.loop(1, NB)
     def _(k):
         in_copy(k).start()
 
-    grad = ug_own[...]
-    for k in range(1, NB):
-        unit_copy(k).wait_recv()
-        grad = grad + ug_recv[k].astype(F32)
-    grad = grad.T
-    f = proto[aligned(b, CC), :].astype(F32)
-    inv = lax.rsqrt(jnp.sum(f * f, axis=1, keepdims=True) + norm_eps)
-    along = jnp.sum(f * grad, axis=1, keepdims=True)
-    grad = (inv * grad - f * (inv * inv * inv) * along).astype(BF16)
-    gp_send[...] = grad
-    gproto[aligned(b, CC), :] = grad
-
-    def proto_copy(k, owner):
-        return copy(gp_send, gproto.at[aligned(owner, CC), :], gp_sem, k, batch_peer(k))
-
-    @pl.loop(1, NB // 2)
-    def _(k):
-        proto_copy(k, b).start()
+    def second_a(k):
+        return copy(sa_send.at[k], sa_recv.at[k], up_sem.at[2], k, z_peer(k))
+
+    def second_b(k):
+        return copy(sb_send.at[k], sb_recv.at[k], up_sem.at[3], k, y_peer(k))
+
+    @pl.loop(1, 4)
+    def _(k):
+        first_a(k).wait_recv()
+        first_b(k).wait_recv()
+
+    def sum_a(i):
+        return (ua_own[i] + ua_recv[1, i].astype(F32)) + (ua_recv[2, i].astype(F32) + ua_recv[3, i].astype(F32))
+
+    def sum_b(i):
+        return (ub_own[i] + ub_recv[1, i].astype(F32)) + (ub_recv[2, i].astype(F32) + ub_recv[3, i].astype(F32))
+
+    @pl.loop(1, 4)
+    def _(k):
+        sa_send[k] = sum_a(lax.rem(z + k, 4)).astype(BF16)
+        second_a(k).start()
+        sb_send[k] = sum_b(lax.rem(y + k, 4)).astype(BF16)
+        second_b(k).start()
+
+    ua_own[z] = sum_a(z)
+    ub_own[y] = sum_b(y)
 
     go = dot_tl(hidden[...], d_raw[...]).reshape(NB, H // NB, Z)
     go_f[...] = go
@@ -406,20 +440,120 @@
     def _(k):
         in_copy(k).wait_recv()
 
-    total = gi_f[b // 2, :, half(b)]
+    total = gi_f[b // 2, b % 2]
     for k in range(1, NB):
         total = total + gi_recv[k].astype(F32)
     total = total.astype(BF16)
     gx_send[...] = total
-    gin[part_of, b // 2, :, half(b)] = total
-
-    def along_x(k, owner):
-        peer = (b, lax.rem(x + k, 4) * 2 + core)
-        return copy(gx_send, gin.at[core * 4 + owner, b // 2, :, half(b)], gx_sem, k, peer)
-
-    @pl.loop(1, 4)
-    def _(k):
-        along_x(k, x).start()
+
+    def tile(q, h):
+        return pl.ds(pl.multiple_of((q % 2 + 2 * h) * 128, 128), 128)
+
+    gin[part_of, b // 2, :, tile(b, 0)] = total[:, :128]
+    gin[part_of, b // 2, :, tile(b, 1)] = total[:, 128:]
+
+    def x_peer(k):
+        return (b, lax.rem(x + k, 4) * 2 + core)
+
+    other_core = (b, x * 2 + 1 - core)
+
+    def a_along_x(k, owner):
+        return copy(gx_send.at[:, pl.ds(0, 128)], gin.at[core * 4 + owner, b // 2, :, tile(b, 0)], ax_sem, k, x_peer(k))
+
+    def b_along_batch(k, q):
+        return copy(gx_send.at[:, pl.ds(128, 128)], gin.at[part_of, q // 2, :, tile(q, 1)], bb_sem, k, batch_peer(k))
+
+    @pl.loop(1, 4)
+    def _(k):
+        a_along_x(k, x).start()
+
+    @pl.loop(1, NB)
+    def _(k):
+        b_along_batch(k, b).start()
+
+    @pl.loop(1, 4)
+    def _(k):
+        second_a(k).wait_recv()
+        second_b(k).wait_recv()
+
+    def finish_proto(own, recv, h):
+        grad = own
+        for k in range(1, 4):
+            grad = grad + recv[k].astype(F32)
+        grad = grad.T
+        f = proto[aligned(b * 2 + h, Z), :].astype(F32)
+        inv = lax.rsqrt(jnp.sum(f * f, axis=1, keepdims=True) + norm_eps)
+        along = jnp.sum(f * grad, axis=1, keepdims=True)
+        gproto[y, z, h] = (inv * grad - f * (inv * inv * inv) * along).astype(BF16)
+
+    finish_proto(ua_own[z], sa_recv, 0)
+    finish_proto(ub_own[y], sb_recv, 1)
+
+    def third_a(k, i):
+        return copy(gproto.at[y, i, 0], gproto.at[y, i, 0], up_sem.at[4], k, z_peer(k))
+
+    def third_b(k, i):
+        return copy(gproto.at[i, z, 1], gproto.at[i, z, 1], up_sem.at[5], k, y_peer(k))
+
+    @pl.loop(1, 4)
+    def _(k):
+        third_a(k, z).start()
+        third_b(k, y).start()
+
+    @pl.loop(1, 4)
+    def _(k):
+        a_along_x(k, back(x, k)).wait_recv()
+
+    def a_plane(q, c):
+        return gin.at[pl.ds(c * 4, 4), q // 2, :, tile(q, 0)]
+
+    def a_along_batch(k, q):
+        return copy(a_plane(q, core), a_plane(q, core), ab_sem, k, batch_peer(k))
+
+    def a_to_core(k, c):
+        q = batch_source(k)
+        return copy(a_plane(q, c), a_plane(q, c), ac_sem, k, other_core)
+
+    @pl.loop(1, NB)
+    def _(k):
+        a_along_batch(k, b).start()
+
+    a_to_core(0, core).start()
+
+    def b_slab(i, c):
+        return gin.at[c * 4 + i, :, :, pl.ds(256, 256)]
+
+    def b_along_x(k, i):
+        return copy(b_slab(i, core), b_slab(i, core), bx_sem, k, x_peer(k))
+
+    def b_to_core(k, c):
+        return copy(b_slab(back(x, k), c), b_slab(back(x, k), c), bc_sem, k, other_core)
+
+    @pl.loop(1, NB)
+    def _(k):
+        b_along_batch(k, batch_source(k)).wait_recv()
+
+    @pl.loop(1, 4)
+    def _(k):
+        b_along_x(k, x).start()
+
+    b_to_core(0, core).start()
+
+    @pl.loop(1, 4)
+    def _(k):
+        third_a(k, back(z, k)).wait_recv()
+        third_b(k, back(y, k)).wait_recv()
+
+    def fourth_a(k, i):
+        return copy(gproto.at[i, :, 0], gproto.at[i, :, 0], up_sem.at[6], k, y_peer(k))
+
+    def fourth_b(k, i):
+        return copy(gproto.at[:, i, 1], gproto.at[:, i, 1], up_sem.at[7], k, z_peer(k))
+
+    @pl.loop(1, 4)
+    def _(k):
+        fourth_a(k, y).start()
+        fourth_b(k, z).start()
 
     total = go_f[b]
     for k in range(1, NB):
@@ -436,52 +570,36 @@
     def _(k):
         out_all(k, b).start()
 
-    @pl.loop(1, 4)
-    def _(k):
-        along_x(k, lax.rem(x + 4 - k, 4)).wait_recv()
-
-    def plane(q, c):
-        return gin.at[pl.ds(c * 4, 4), q // 2, :, half(q)]
-
-    def along_batch(k, owner):
-        return copy(plane(owner, core), plane(owner, core), gb_sem, k, batch_peer(k))
-
-    @pl.loop(1, NB)
-    def _(k):
-        along_batch(k, b).start()
-
-    @pl.loop(NB // 2, NB)
-    def _(k):
-        proto_copy(k, b).start()
-
-    def to_core(k, c):
-        q = batch_source(k)
-        return copy(plane(q, c), plane(q, c), gc_sem, k, (b, x * 2 + 1 - core))
-
-    to_core(0, core).start()
-
-    @pl.loop(1, NB)
-    def _(k):
-        along_batch(k, batch_source(k)).wait_recv()
-        to_core(k, core).start()
+    @pl.loop(1, NB)
+    def _(k):
+        a_along_batch(k, batch_source(k)).wait_recv()
+        a_to_core(k, core).start()
+
+    @pl.loop(1, 4)
+    def _(k):
+        b_along_x(k, back(x, k)).wait_recv()
+        b_to_core(k, core).start()
 
     @pl.loop(0, NB)
     def _(k):
-        to_core(k, 1 - core).wait_recv()
-        to_core(k, core).wait_send()
-
-    @pl.loop(1, NB)
-    def _(k):
-        proto_copy(k, batch_source(k)).wait_recv()
+        a_to_core(k, 1 - core).wait_recv()
+        a_to_core(k, core).wait_send()
+
+    @pl.loop(0, 4)
+    def _(k):
+        b_to_core(k, 1 - core).wait_recv()
+        b_to_core(k, core).wait_send()
+
+    @pl.loop(1, NB)
+    def _(k):
         out_all(k, batch_source(k)).wait_recv()
         for it in range(ITERS):
             copy(col_send.at[it], col_recv.at[it, k], col_sem.at[it], k, batch_peer(k)).wait_send()
-        unit_copy(k).wait_send()
-        proto_copy(k, b).wait_send()
         out_copy(k).wait_send()
         out_all(k, b).wait_send()
         in_copy(k).wait_send()
-        along_batch(k, b).wait_send()
+        a_along_batch(k, b).wait_send()
+        b_along_batch(k, b).wait_send()
 
     @pl.loop(1, NP)
     def _(k):
@@ -492,7 +610,18 @@
 
     @pl.loop(1, 4)
     def _(k):
-        along_x(k, x).wait_send()
+        fourth_a(k, back(y, k)).wait_recv()
+        fourth_b(k, back(z, k)).wait_recv()
+        first_a(k).wait_send()
+        first_b(k).wait_send()
+        second_a(k).wait_send()
+        second_b(k).wait_send()
+        third_a(k, z).wait_send()
+        third_b(k, y).wait_send()
+        fourth_a(k, y).wait_send()
+        fourth_b(k, z).wait_send()
+        a_along_x(k, x).wait_send()
+        b_along_x(k, x).wait_send()
 
 
 def body(embeddings, pairing, w_in, w_out, prototypes):
@@ -503,7 +632,7 @@
     grad_in, grad_out, grad_proto = pl.pallas_call(
         kernel,
         name="swav_step",
-        out_shape=(out(NP, 8, 16, H), out(NB, H // NB, Z), out(W, Z)),
+        out_shape=(out(NP, 8, 16, H), out(NB, H // NB, Z), out(4, 4, 2, Z, Z)),
         in_specs=[vmem] * 5,
         out_specs=(vmem,) * 3,
         scratch_shapes=[
@@ -514,11 +643,13 @@
             v((ITERS + 1, 8, 128), F32), v((ITERS + 1, NP, 8, 128), F32),
             v((R, Z), BF16), v((NP, RC, Z), BF16), v((NP, RC, Z), BF16), v((RC, Z), F32),
             v((RC, Z), BF16), v((R, Z), BF16), v((R, Z), BF16), v((R, H), BF16),
-            v((NB, Z, CC), BF16), v((NB, Z, CC), BF16), v((Z, CC), F32), v((CC, Z), BF16),
+            v((4, 4, Z, Z), BF16), v((4, 4, Z, Z), BF16), v((4, Z, Z), F32),
+            v((4, 4, Z, Z), BF16), v((4, 4, Z, Z), BF16), v((4, Z, Z), F32),
+            v((4, Z, Z), BF16), v((4, Z, Z), BF16), v((4, Z, Z), BF16), v((4, Z, Z), BF16),
             v((NB, H // NB, Z), F32), v((NB, H // NB, Z), BF16), v((NB, H // NB, Z), BF16), v((H // NB, Z), BF16),
-            v((8, 16, H), F32), v((8, 16, H), BF16), v((NB, 16, 256), BF16), v((16, 256), BF16),
-            dma(ITERS, 2, NB), dma(ITERS + 1, 2, NP), dma(2, NP), dma(2, NP), dma(2, NB), dma(2, NB),
-            dma(2, NB), dma(2, NB), dma(2, NB), dma(2, 4), dma(2, NB), dma(2, NB),
+            v((8, 2, 16, 256), F32), v((8, 2, 16, 256), BF16), v((NB, 16, 256), BF16), v((16, 256), BF16),
+            dma(ITERS, 2, NB), dma(ITERS + 1, 2, NP), dma(2, NP), dma(2, NP), dma(8, 2, 4),
+            dma(2, NB), dma(2, NB), dma(2, NB), dma(2, 4), dma(2, NB), dma(2, NB), dma(2, NB), dma(2, 4), dma(2, 4),
         ],
         compiler_params=pltpu.CompilerParams(
             collective_id=0, has_side_effects=True, vmem_limit_bytes=60 << 20
@@ -527,7 +658,7 @@
     return (
         grad_in.reshape(E, H).astype(F32),
         grad_out.reshape(H, Z).astype(F32),
-        grad_proto.astype(F32),
+        grad_proto.reshape(W, Z).astype(F32),
     )
 
 

time: 126 us -> 112 us (0.89)
  Pallas kernels: 120 us -> 106 us
    pallas_call x1, Pallas kernels: 120 us -> 106 us  [body(): pl.pallas_call(kernel, name='swav_step', out_shape=(out(NP, 8, 16, H), ou...]
    convert_element_type x1, other arithmetic: 1.46 us -> 2.77 us  [body(): grad_proto.reshape(W, Z).astype(F32)]
where the time goes in v3:
time: 112 us
  Pallas kernels  106 us (95%)
  other arithmetic  5.18 us (5%)
    pallas_call x1, Pallas kernels, body(): pl.pallas_call(kernel, name='swav_step', out_shape=(out(NP, 8, 16, H), ou...  106 us
    convert_element_type x1, other arithmetic, body(): grad_proto.reshape(W, Z).astype(F32)  2.77 us

profile of v3, /device:TPU:0, one launch (start us, length us, event | category | flops | bytes accessed | tf_op | source)
XLA Modules:
  0.0 111.7 jit_solution(13816221152271934101)
XLA Ops:
  0.6 105.9 %swav_step.1 = (bf16[8,8,16,512]{3,2,1,0:T(8,128)(2,1)}, bf16[16,32,128]{2,1,0:T(8,128)(2,1)}, bf16[4,4,2,128,128]{4,3,2,1,0:T(8,128)(2,1)}) custom-call(bf16[1024,1024]{1,0:T(8,128)(2,1)} %emb.1, s32[8,128]{1,0:T(8,128)} %bitcast.10, bf16[1024,512]{1,0:T(8,128)(2,1)} %w_in.1, bf16[512,128]{1,0:T(8,128)(2,1)} %w_out.1, bf16[4096,128]{1,0:T(8,128)(2,1)} %proto.1), custom_call_target="tpu_custom_call" | custom-call | tf_op jit(solution)/shard_map/swav_step/pallas_call | solution.py:632
  106.5 0.0 copy-start
  106.5 2.8 %bitcast_convert_fusion = f32[4096,128]{1,0:T(8,128)} fusion(bf16[4,4,2,128,128]{4,3,2,1,0:T(8,128)(2,1)} %get-tuple-element.8), kind=kLoop, calls=%fused_computation | loop fusion | flops 524288 | bytes 3145728 | tf_op jit(solution)/shard_map/convert_element_type | solution.py:661
  109.3 0.0 copy-start.1
  109.3 0.0 copy-done
  109.3 1.7 %bitcast_convert_fusion.1 = f32[1024,512]{1,0:T(8,128)} fusion(bf16[8,8,16,512]{3,2,1,0:T(8,128)(2,1)S(1)} %copy-done), kind=kLoop, calls=%fused_computation.1 | loop fusion | flops 524288 | bytes 3145728 | tf_op jit(solution)/shard_map/convert_element_type | solution.py:659
  111.0 0.0 copy-done.1
  111.0 0.7 bitcast_convert_fusion.2
Async XLA Ops:
  106.5 2.8 %copy-start = (bf16[8,8,16,512]{3,2,1,0:T(8,128)(2,1)S(1)}, bf16[8,8,16,512]{3,2,1,0:T(8,128)(2,1)}, u32[]{:S(2)}) copy-start(bf16[8,8,16,512]{3,2,1,0:T(8,128)(2,1)} %get-tuple-element.6) | copy-start | bytes 3145732
  109.3 1.7 %copy-start.1 = (bf16[16,32,128]{2,1,0:T(8,128)(2,1)S(1)}, bf16[16,32,128]{2,1,0:T(8,128)(2,1)}, u32[]{:S(2)}) copy-start(bf16[16,32,128]{2,1,0:T(8,128)(2,1)} %get-tuple-element.7) | copy-start | bytes 393220

commit v4 on v3

--- a/solution.py
+++ b/solution.py
@@ -52,15 +52,15 @@
 
 
 def kernel(
-    emb, pairing, w_in, w_out, proto,
+    emb_hbm, pairing, w_in_hbm, w_out_hbm, proto,
     gin, gout, gproto,
-    pre, hidden, raw, perm, perm_t, views, views_t, unit, eh, dsc,
-    tot_acc, row_b, tot_b, raw_own, c_ref,
-    col_line, col_send, col_recv, row_send, row_recv,
+    emb, w_in, w_out, pre, hidden, raw, perm, perm_t, views, views_t, unit, eh, dsc,
+    tot_acc, row_b, row_n, tot_b, raw_own, c_ref,
+    col_acc, col_line, col_send, col_recv, row_send, row_recv,
     vun, vg_send, vg_recv, vg_own, dr_send, dr_all, d_raw, d_pre,
     ua_send, ua_recv, ua_own, ub_send, ub_recv, ub_own, sa_send, sa_recv, sb_send, sb_recv,
     go_f, go_send, go_recv, goa_send, gi_f, gi_send, gi_recv, gx_send,
-    col_sem, row_sem, vg_sem, dr_sem, up_sem, go_sem, goa_sem, gi_sem, ax_sem, ab_sem, ac_sem, bb_sem, bx_sem, bc_sem,
+    col_sem, row_sem, vg_sem, dr_sem, up_sem, go_sem, goa_sem, gi_sem, ax_sem, ab_sem, ac_sem, bb_sem, bx_sem, bc_sem, in_sem,
 ):
     b = lax.axis_index("batch")
     p = lax.axis_index("proto")
@@ -85,6 +85,13 @@
             device_id=device, device_id_type=MESH,
         )
 
+    loads = [
+        pltpu.make_async_copy(src, dst, in_sem.at[i])
+        for i, (src, dst) in enumerate(((emb_hbm, emb), (w_in_hbm, w_in), (w_out_hbm, w_out)))
+    ]
+    for load in loads:
+        load.start()
+
     barrier = pltpu.get_barrier_semaphore()
 
     @pl.loop(1, NB)
@@ -94,18 +101,6 @@
     @pl.loop(1, NP)
     def _(k):
         pl.semaphore_signal(barrier, inc=1, device_id=proto_peer(k), device_id_type=MESH)
-
-    @pl.loop(0, R // 256)
-    def _(i):
-        rows = aligned(i, 256)
-        v = dot(emb[rows, :], w_in[...])
-        pre[rows, :] = v
-        hid = (0.5 * v * (1.0 + jnp.tanh(gelu_a * (v + gelu_b * (v * v * v))))).astype(BF16)
-        hidden[rows, :] = hid
-        out = dot(hid, w_out[...])
-        raw[rows, :] = out
-        inv = lax.rsqrt(jnp.sum(out * out, axis=1, keepdims=True) + norm_eps)
-        vun[rows, :] = (out * inv).astype(BF16)
 
     mate = pairing[...]
     lead = mate > iota((8, 128), 0) * 128 + iota((8, 128), 1)
@@ -135,8 +130,6 @@
     def _(i):
         perm[aligned(i, 128), :] = onehot(pos == iota((128, R), 0) + i * 128)
 
-    views[...] = dot(perm[...], vun[...]).astype(BF16)
-
     @pl.loop(0, W // 256)
     def _(i):
         rows = aligned(i, 256)
@@ -144,10 +137,132 @@
         inv = lax.rsqrt(jnp.sum(f * f, axis=1, keepdims=True) + norm_eps)
         unit[rows, :] = (f * inv).astype(BF16)
 
+    for load in loads:
+        load.wait()
+
+    @pl.loop(0, R // 256)
+    def _(i):
+        rows = aligned(i, 256)
+        v = dot(emb[rows, :], w_in[...])
+        pre[rows, :] = v
+        hid = (0.5 * v * (1.0 + jnp.tanh(gelu_a * (v + gelu_b * (v * v * v))))).astype(BF16)
+        hidden[rows, :] = hid
+        out = dot(hid, w_out[...])
+        raw[rows, :] = out
+        inv = lax.rsqrt(jnp.sum(out * out, axis=1, keepdims=True) + norm_eps)
+        vun[rows, :] = (out * inv).astype(BF16)
+
+    views[...] = dot(perm[...], vun[...]).astype(BF16)
+
+    def column_copy(it, h, k):
+        return copy(col_send.at[it, h], col_recv.at[it, h, k], col_sem.at[it, h], k, batch_peer(k))
+
+    def start_columns(it, h):
+        col_send[it, h] = col_line[h * 16 : h * 16 + 16, :].astype(BF16)
+
+        @pl.loop(1, NB)
+        def _(k):
+            column_copy(it, h, k).start()
+
+    def finish_columns(it, h):
+        @pl.loop(1, NB)
+        def _(k):
+            column_copy(it, h, k).wait_recv()
+
+        total = col_send[it, h].astype(F32)
+        for k in range(1, NB):
+            total = total + col_recv[it, h, k].astype(F32)
+        c_ref[h * 16 : h * 16 + 16, :] = 1.0 / total
+
+    def row_copy(slot, k):
+        return copy(row_send.at[slot], row_recv.at[slot, k], row_sem.at[slot], k, proto_peer(k))
+
+    def start_rows(slot, src, first, count):
+        for q in range(count):
+            at = (first + q) * 128
+            row_send[slot, q : q + 1, :] = jnp.sum(src[at : at + 128, :].T, axis=0, keepdims=True)
+
+        @pl.loop(1, NP)
+        def _(k):
+            row_copy(slot, k).start()
+
+    def finish_rows(slot):
+        @pl.loop(1, NP)
+        def _(k):
+            row_copy(slot, k).wait_recv()
+
+        total = row_send[slot]
+        for k in range(1, NP):
+            total = total + row_recv[slot, k]
+        return 1.0 / total
+
+    def spread(lines, dst, first, count):
+        for q in range(count):
+            at = (first + q) * 128
+            dst[at : at + 128, :] = jnp.broadcast_to(lines[q : q + 1, :], (128, 128)).T.astype(dst.dtype)
+
+    def pairwise(terms):
+        while len(terms) > 1:
+            terms = [terms[m] + terms[m + 1] for m in range(0, len(terms), 2)]
+        return terms[0]
+
+    def column_sweep(it, rows_half):
+        for h in range(2):
+            lines = range(h * 16, h * 16 + 16)
+
+            def some_rows(i, acc):
+                rows = [pl.ds(pl.multiple_of(i * 64 + m * 16, 16), 16) for m in range(4)]
+                r = [row_n[at, :] for at in rows]
+                out = []
+                for j, a in zip(lines, acc):
+                    part = pairwise([dsc[rows[m], j * 128 : j * 128 + 128] * r[m] for m in range(4)]).astype(F32)
+                    out.append(a + (part[0:8] + part[8:16]))
+                return tuple(out)
+
+            if rows_half == 0:
+                acc = tuple(jnp.zeros((8, 128), F32) for _ in lines)
+            else:
+                acc = tuple(col_acc[:, j * 128 : j * 128 + 128] for j in lines)
+            acc = lax.fori_loop(rows_half * 8, rows_half * 8 + 8, some_rows, acc)
+            if rows_half == 0:
+                for j, a in zip(lines, acc):
+                    col_acc[:, j * 128 : j * 128 + 128] = a
+            else:
+                for j, a in zip(lines, acc):
+                    col_line[j : j + 1, :] = jnp.sum(a, axis=0, keepdims=True)
+                start_columns(it, h)
+
+    def row_sweep(h, first, last):
+        lines = range(h * 16, h * 16 + 16)
+        c = [jnp.broadcast_to(c_ref[j : j + 1, :], (16, 128)).astype(BF16) for j in lines]
+
+        @pl.loop(first // 16, last // 16)
+        def _(i):
+            rows = aligned(i, 16)
+            parts = []
+            for g in range(0, 16, 4):
+                some = [dsc[rows, (h * 16 + g + m) * 128 : (h * 16 + g + m + 1) * 128] * c[g + m] for m in range(4)]
+                parts.append(pairwise(some).astype(F32))
+            total = pairwise(parts)
+            row_b[rows, :] = total if h == 0 else row_b[rows, :] + total
+
+    def rows_of(it):
+        finish_columns(it, 0)
+        row_sweep(0, 0, R)
+        finish_columns(it, 1)
+        for h in range(2):
+            row_sweep(1, h * 512, h * 512 + 512)
+            start_rows(it * 2 + h, row_b, h * 4, 4)
+
+    def columns_of(it):
+        for h in range(2):
+            spread(finish_rows(it * 2 - 2 + h), row_n, h * 4, 4)
+            column_sweep(it, h)
+
     tot_acc[...] = jnp.zeros_like(tot_acc)
-
-    @pl.loop(0, W // 512)
-    def _(j):
+    row_send[...] = jnp.zeros_like(row_send)
+
+    def some_columns(j):
         cols = aligned(j, 512)
         u = unit[cols, :]
 
@@ -156,85 +271,22 @@
             e = jnp.exp2(dot_t(views[rows, :], u) * half_log2)
             eh[rows, cols] = e
             tot_acc[rows, :] += (e[:, 0:128] + e[:, 128:256]) + (e[:, 256:384] + e[:, 384:512])
-            return acc + jnp.sum((e * e).reshape(16, 8, 512), axis=0)
+            e = e * e
+            dsc[rows, cols] = e.astype(BF16)
+            return acc + jnp.sum(e.reshape(16, 8, 512), axis=0)
 
         acc = lax.fori_loop(0, R // 128, some_rows, jnp.zeros((8, 512), F32), unroll=8)
         line = jnp.sum(acc, axis=0, keepdims=True)
         for m in range(4):
             col_line[pl.ds(j * 4 + m, 1), :] = line[:, m * 128 : m * 128 + 128]
 
+    pl.loop(0, 4)(some_columns)
     pl.semaphore_wait(barrier, NB - 1 + NP - 1)
-
-    def start_columns(it):
-        col_send[it] = col_line[...].astype(BF16)
-
-        @pl.loop(1, NB)
-        def _(k):
-            copy(col_send.at[it], col_recv.at[it, k], col_sem.at[it], k, batch_peer(k)).start()
-
-    def finish_columns(it):
-        @pl.loop(1, NB)
-        def _(k):
-            copy(col_send.at[it], col_recv.at[it, k], col_sem.at[it], k, batch_peer(k)).wait_recv()
-
-        total = col_send[it].astype(F32)
-        for k in range(1, NB):
-            total = total + col_recv[it, k].astype(F32)
-        c_ref[...] = 1.0 / total
-
-    def start_rows(slot):
-        @pl.loop(1, NP)
-        def _(k):
-            copy(row_send.at[slot], row_recv.at[slot, k], row_sem.at[slot], k, proto_peer(k)).start()
-
-    def finish_rows(slot):
-        @pl.loop(1, NP)
-        def _(k):
-            copy(row_send.at[slot], row_recv.at[slot, k], row_sem.at[slot], k, proto_peer(k)).wait_recv()
-
-        total = row_send[slot]
-        for k in range(1, NP):
-            total = total + row_recv[slot, k]
-        return 1.0 / total
-
-    def to_lines(src, slot):
-        for q in range(8):
-            row_send[slot, q : q + 1, :] = jnp.sum(src[q * 128 : q * 128 + 128, :].T, axis=0, keepdims=True)
-
-    def spread(lines, dst):
-        for q in range(8):
-            dst[q * 128 : q * 128 + 128, :] = jnp.broadcast_to(lines[q : q + 1, :], (128, 128)).T
-
-    def column_sweep():
-        def some_rows(i, acc):
-            rows = aligned(i, 8)
-            r = row_b[rows, :]
-            out = []
-            for j in range(WV):
-                e = eh[rows, j * 128 : j * 128 + 128]
-                out.append(acc[j] + (e * e) * r)
-            return tuple(out)
-
-        acc = lax.fori_loop(0, R // 8, some_rows, tuple(jnp.zeros((8, 128), F32) for _ in range(WV)))
-        for j in range(WV):
-            col_line[j : j + 1, :] = jnp.sum(acc[j], axis=0, keepdims=True)
-
-    def row_sweep():
-        c = [jnp.broadcast_to(c_ref[j : j + 1, :], (8, 128)) for j in range(WV)]
-
-        @pl.loop(0, R // 8)
-        def _(i):
-            rows = aligned(i, 8)
-            part = [jnp.zeros((8, 128), F32) for _ in range(4)]
-            for j in range(WV):
-                e = eh[rows, j * 128 : j * 128 + 128]
-                part[j % 4] = part[j % 4] + (e * e) * c[j]
-            row_b[rows, :] = (part[0] + part[1]) + (part[2] + part[3])
-
-    start_columns(0)
-
-    to_lines(tot_acc, ITERS)
-    start_rows(ITERS)
+    start_columns(0, 0)
+    pl.loop(4, 8)(some_columns)
+    start_columns(0, 1)
+
+    start_rows(2 * ITERS, tot_acc, 0, 8)
     views_t[...] = views[...].astype(F32).T.astype(BF16)
 
     @pl.loop(0, R // 256)
@@ -244,21 +296,14 @@
         t = jnp.tanh(gelu_a * (v + gelu_b * (v * v * v)))
         pre[rows, :] = 0.5 * (1.0 + t) + 0.5 * v * (1.0 - t * t) * (gelu_a * (1.0 + 3.0 * gelu_b * (v * v)))
 
-    finish_columns(0)
-    row_sweep()
-    to_lines(row_b, 0)
-    start_rows(0)
-
+    rows_of(0)
     for q in range(8):
         at = jnp.broadcast_to(pos[:, q * 128 : q * 128 + 128], (128, 128)).astype(F32).T
         for k in range(8):
             here = (iota((128, 128), 1) + k * 128).astype(F32)
             perm_t[q * 128 : q * 128 + 128, k * 128 : k * 128 + 128] = onehot(at == here)
 
-    spread(finish_rows(0), row_b)
-    column_sweep()
-    start_columns(1)
-
+    columns_of(1)
     own = perm[aligned(p, RC), :]
     r0 = raw[...]
     r1 = r0.astype(BF16)
@@ -266,28 +311,15 @@
     r2 = r0.astype(BF16)
     r3 = (r0 - r2.astype(F32)).astype(BF16)
     raw_own[...] = dot(own, r1) + dot(own, r2) + dot(own, r3)
-    spread(finish_rows(ITERS) * loss_gain, tot_b)
-
-    finish_columns(1)
-    row_sweep()
-    to_lines(row_b, 1)
-    start_rows(1)
-    spread(finish_rows(1), row_b)
-    column_sweep()
-    start_columns(2)
-    finish_columns(2)
-    row_sweep()
-    to_lines(row_b, 2)
-    start_rows(2)
-    spread(finish_rows(2) * loss_gain, row_b)
+    spread(finish_rows(2 * ITERS) * loss_gain, tot_b, 0, 8)
+    rows_of(1)
+    columns_of(2)
+    rows_of(2)
 
     def view_copy(k):
         return copy(vg_send.at[k], vg_recv.at[k], vg_sem, k, proto_peer(k))
 
-    @pl.loop(1, NP + 1)
-    def _(k):
-        q = lax.rem(p + k, NP)
-
+    def one_chunk(q):
         @pl.loop(0, 4)
         def _(h):
             top, low = aligned(q * 8 + h, 16), aligned(q * 8 + h + 4, 16)
@@ -301,15 +333,23 @@
                 dsc[low, cols] = (e_low * t_low - (e_top * e_top) * c * r_top).astype(BF16)
 
         part = dot(dsc[aligned(q, RC), :], unit[...])
-        vg_send[lax.rem(k, NP)] = part.astype(BF16)
-
-        @pl.when(k < NP)
+        k = lax.rem(q + NP - p, NP)
+        vg_send[k] = part.astype(BF16)
+
+        @pl.when(k > 0)
         def _():
             view_copy(k).start()
 
-        @pl.when(k == NP)
+        @pl.when(k == 0)
         def _():
             vg_own[...] = part
+
+    for h in range(2):
+        spread(finish_rows(2 * ITERS - 2 + h) * loss_gain, row_b, h * 4, 4)
+
+        @pl.loop(1, 5)
+        def _(m):
+            one_chunk(lax.rem(p + m, 4) + h * 4)
 
     def y_peer(k):
         return (lax.rem(y + k, 4) * 4 + z, p)
@@ -594,7 +634,8 @@
     def _(k):
         out_all(k, batch_source(k)).wait_recv()
         for it in range(ITERS):
-            copy(col_send.at[it], col_recv.at[it, k], col_sem.at[it], k, batch_peer(k)).wait_send()
+            column_copy(it, 0, k).wait_send()
+            column_copy(it, 1, k).wait_send()
         out_copy(k).wait_send()
         out_all(k, b).wait_send()
         in_copy(k).wait_send()
@@ -603,8 +644,8 @@
 
     @pl.loop(1, NP)
     def _(k):
-        for slot in range(ITERS + 1):
-            copy(row_send.at[slot], row_recv.at[slot, k], row_sem.at[slot], k, proto_peer(k)).wait_send()
+        for slot in range(2 * ITERS + 1):
+            row_copy(slot, k).wait_send()
         view_copy(k).wait_send()
         raw_copy(k, p).wait_send()
 
@@ -626,21 +667,22 @@
 
 def body(embeddings, pairing, w_in, w_out, prototypes):
     vmem = pl.BlockSpec(memory_space=pltpu.VMEM)
-    out = lambda *shape: jax.ShapeDtypeStruct(shape, BF16)
+    hbm = pl.BlockSpec(memory_space=pl.ANY)
+    out = lambda *shape: pltpu.VMEM(shape, BF16)
     dma = lambda *shape: pltpu.SemaphoreType.DMA(shape)
     v = pltpu.VMEM
     grad_in, grad_out, grad_proto = pl.pallas_call(
         kernel,
         name="swav_step",
         out_shape=(out(NP, 8, 16, H), out(NB, H // NB, Z), out(4, 4, 2, Z, Z)),
-        in_specs=[vmem] * 5,
+        in_specs=[hbm, vmem, hbm, hbm, vmem],
         out_specs=(vmem,) * 3,
         scratch_shapes=[
-            v((R, H), F32), v((R, H), BF16), v((R, Z), F32), v((R, R), BF16), v((R, R), BF16),
+            v((R, E), BF16), v((E, H), BF16), v((H, Z), BF16), v((R, H), F32), v((R, H), BF16), v((R, Z), F32), v((R, R), BF16), v((R, R), BF16),
             v((R, Z), BF16), v((Z, R), BF16), v((W, Z), BF16), v((R, W), F32), v((R, W), BF16),
-            v((R, 128), F32), v((R, 128), F32), v((R, 128), F32), v((RC, Z), F32), v((WV, 128), F32),
-            v((WV, 128), F32), v((ITERS, WV, 128), BF16), v((ITERS, NB, WV, 128), BF16),
-            v((ITERS + 1, 8, 128), F32), v((ITERS + 1, NP, 8, 128), F32),
+            v((R, 128), F32), v((R, 128), F32), v((R, 128), BF16), v((R, 128), F32), v((RC, Z), F32), v((WV, 128), F32),
+            v((8, W), F32), v((WV, 128), F32), v((ITERS, 2, 16, 128), BF16), v((ITERS, 2, NB, 16, 128), BF16),
+            v((2 * ITERS + 1, 8, 128), F32), v((2 * ITERS + 1, NP, 8, 128), F32),
             v((R, Z), BF16), v((NP, RC, Z), BF16), v((NP, RC, Z), BF16), v((RC, Z), F32),
             v((RC, Z), BF16), v((R, Z), BF16), v((R, Z), BF16), v((R, H), BF16),
             v((4, 4, Z, Z), BF16), v((4, 4, Z, Z), BF16), v((4, Z, Z), F32),
@@ -648,8 +690,8 @@
             v((4, Z, Z), BF16), v((4, Z, Z), BF16), v((4, Z, Z), BF16), v((4, Z, Z), BF16),
             v((NB, H // NB, Z), F32), v((NB, H // NB, Z), BF16), v((NB, H // NB, Z), BF16), v((H // NB, Z), BF16),
             v((8, 2, 16, 256), F32), v((8, 2, 16, 256), BF16), v((NB, 16, 256), BF16), v((16, 256), BF16),
-            dma(ITERS, 2, NB), dma(ITERS + 1, 2, NP), dma(2, NP), dma(2, NP), dma(8, 2, 4),
-            dma(2, NB), dma(2, NB), dma(2, NB), dma(2, 4), dma(2, NB), dma(2, NB), dma(2, NB), dma(2, 4), dma(2, 4),
+            dma(ITERS, 2, 2, NB), dma(2 * ITERS + 1, 2, NP), dma(2, NP), dma(2, NP), dma(8, 2, 4),
+            dma(2, NB), dma(2, NB), dma(2, NB), dma(2, 4), dma(2, NB), dma(2, NB), dma(2, NB), dma(2, 4), dma(2, 4), dma(3),
         ],
         compiler_params=pltpu.CompilerParams(
             collective_id=0, has_side_effects=True, vmem_limit_bytes=60 << 20

time: 112 us -> 102 us (0.911)
  Pallas kernels: 106 us -> 97.8 us
  other arithmetic: 5.18 us -> 3.93 us
    pallas_call x1, Pallas kernels: 106 us -> 97.8 us  [body(): pl.pallas_call(kernel, name='swav_step', out_shape=(out(NP, 8, 16, H), ou...]
    convert_element_type x1, other arithmetic: 2.77 us -> 1.52 us  [body(): grad_proto.reshape(W, Z).astype(F32)]
where the time goes in v4:
time: 102 us
  Pallas kernels  97.8 us (96%)
  other arithmetic  3.93 us (4%)
    pallas_call x1, Pallas kernels, body(): pl.pallas_call(kernel, name='swav_step', out_shape=(out(NP, 8, 16, H), ou...  97.8 us

profile of v4, /device:TPU:0, one launch (start us, length us, event | category | flops | bytes accessed | tf_op | source)
XLA Modules:
  0.0 102.3 jit_solution(12171580172844448878)
XLA Ops:
  0.6 97.8 %swav_step.1 = (bf16[8,8,16,512]{3,2,1,0:T(8,128)(2,1)S(1)}, bf16[16,32,128]{2,1,0:T(8,128)(2,1)S(1)}, bf16[4,4,2,128,128]{4,3,2,1,0:T(8,128)(2,1)S(1)}) custom-call(bf16[1024,1024]{1,0:T(8,128)(2,1)} %emb_hbm.1, s32[8,128]{1,0:T(8,128)} %bitcast.10, bf16[1024,512]{1,0:T(8,128)(2,1)} %w_in_hbm.1, bf16[512,128]{1,0:T(8,128)(2,1)} %w_out_hbm.1, ...), custom_call_target="tpu_custom_call" | custom-call | tf_op jit(solution)/shard_map/swav_step/pallas_call | solution.py:674
  98.4 1.5 %bitcast_convert_fusion = f32[4096,128]{1,0:T(8,128)} fusion(bf16[4,4,2,128,128]{4,3,2,1,0:T(8,128)(2,1)S(1)} %get-tuple-element.8), kind=kLoop, calls=%fused_computation | loop fusion | flops 524288 | bytes 3145728 | tf_op jit(solution)/shard_map/convert_element_type | solution.py:703
  99.9 1.7 %bitcast_convert_fusion.1 = f32[1024,512]{1,0:T(8,128)} fusion(bf16[8,8,16,512]{3,2,1,0:T(8,128)(2,1)S(1)} %get-tuple-element.6), kind=kLoop, calls=%fused_computation.1 | loop fusion | flops 524288 | bytes 3145728 | tf_op jit(solution)/shard_map/convert_element_type | solution.py:701
  101.6 0.7 bitcast_convert_fusion.2

commit v5 on v4

--- a/solution.py
+++ b/solution.py
@@ -130,13 +130,6 @@
     def _(i):
         perm[aligned(i, 128), :] = onehot(pos == iota((128, R), 0) + i * 128)
 
-    @pl.loop(0, W // 256)
-    def _(i):
-        rows = aligned(i, 256)
-        f = proto[rows, :].astype(F32)
-        inv = lax.rsqrt(jnp.sum(f * f, axis=1, keepdims=True) + norm_eps)
-        unit[rows, :] = (f * inv).astype(BF16)
-
     for load in loads:
         load.wait()
 
@@ -151,6 +144,11 @@
         raw[rows, :] = out
         inv = lax.rsqrt(jnp.sum(out * out, axis=1, keepdims=True) + norm_eps)
         vun[rows, :] = (out * inv).astype(BF16)
+        for m in range(8):
+            some = aligned(i * 8 + m, 128)
+            f = proto[some, :].astype(F32)
+            inv = lax.rsqrt(jnp.sum(f * f, axis=1, keepdims=True) + norm_eps)
+            unit[some, :] = (f * inv).astype(BF16)
 
     views[...] = dot(perm[...], vun[...]).astype(BF16)
 
@@ -371,16 +369,16 @@
         k = lax.rem(kk, 4)
         to_y = lax.rem(y + k, 4)
 
-        @pl.loop(0, 4)
-        def _(m):
-            to_z = lax.rem(z + m, 4)
-            part = dot(views_t[...], dsc[:, aligned(to_y * 4 + to_z, CC)])
-            ua_send[k, to_z] = part[:, :Z].astype(BF16)
+        parts = dot(views_t[...], dsc[:, aligned(to_y, 4 * CC)])
+        for i in range(4):
+            part = parts[:, i * CC : i * CC + CC]
+            m = back(i, z)
+            ua_send[k, i] = part[:, :Z].astype(BF16)
             ub_send[m, to_y] = part[:, Z:].astype(BF16)
 
             @pl.when(k == 0)
             def _():
-                ua_own[to_z] = part[:, :Z]
+                ua_own[i] = part[:, :Z]
 
             @pl.when(m == 0)
             def _():
@@ -438,6 +436,17 @@
     def _(k):
         in_copy(k).start()
 
+    go = dot_tl(hidden[...], d_raw[...]).reshape(NB, H // NB, Z)
+    go_f[...] = go
+    go_send[...] = go.astype(BF16)
+
+    def out_copy(k):
+        return copy(go_send.at[lax.rem(b + k, NB)], go_recv.at[k], go_sem, k, batch_peer(k))
+
+    @pl.loop(1, NB)
+    def _(k):
+        out_copy(k).start()
+
     def second_a(k):
         return copy(sa_send.at[k], sa_recv.at[k], up_sem.at[2], k, z_peer(k))
 
@@ -464,17 +473,6 @@
 
     ua_own[z] = sum_a(z)
     ub_own[y] = sum_b(y)
-
-    go = dot_tl(hidden[...], d_raw[...]).reshape(NB, H // NB, Z)
-    go_f[...] = go
-    go_send[...] = go.astype(BF16)
-
-    def out_copy(k):
-        return copy(go_send.at[lax.rem(b + k, NB)], go_recv.at[k], go_sem, k, batch_peer(k))
-
-    @pl.loop(1, NB)
-    def _(k):
-        out_copy(k).start()
 
     @pl.loop(1, NB)
     def _(k):
@@ -510,6 +508,21 @@
     @pl.loop(1, NB)
     def _(k):
         b_along_batch(k, b).start()
+
+    total = go_f[b]
+    for k in range(1, NB):
+        out_copy(k).wait_recv()
+        total = total + go_recv[k].astype(F32)
+    total = total.astype(BF16)
+    goa_send[...] = total
+    gout[b] = total
+
+    def out_all(k, owner):
+        return copy(goa_send, gout.at[owner], goa_sem, k, batch_peer(k))
+
+    @pl.loop(1, NB)
+    def _(k):
+        out_all(k, b).start()
 
     @pl.loop(1, 4)
     def _(k):
@@ -594,21 +607,6 @@
     def _(k):
         fourth_a(k, y).start()
         fourth_b(k, z).start()
-
-    total = go_f[b]
-    for k in range(1, NB):
-        out_copy(k).wait_recv()
-        total = total + go_recv[k].astype(F32)
-    total = total.astype(BF16)
-    goa_send[...] = total
-    gout[b] = total
-
-    def out_all(k, owner):
-        return copy(goa_send, gout.at[owner], goa_sem, k, batch_peer(k))
-
-    @pl.loop(1, NB)
-    def _(k):
-        out_all(k, b).start()
 
     @pl.loop(1, NB)
     def _(k):

time: 102 us -> 99.2 us (0.973)
  Pallas kernels: 97.8 us -> 94.4 us
    pallas_call x1, Pallas kernels: 97.8 us -> 94.4 us  [body(): pl.pallas_call(kernel, name='swav_step', out_shape=(out(NP, 8, 16, H), ou...]
where the time goes in v5:
time: 99.2 us; the launch traced here: 99 us
  Pallas kernels  94.4 us (95%)
  other arithmetic  3.93 us (4%)
    pallas_call x1, Pallas kernels, body(): pl.pallas_call(kernel, name='swav_step', out_shape=(out(NP, 8, 16, H), ou...  94.4 us

profile of v5, /device:TPU:0, one launch (start us, length us, event | category | flops | bytes accessed | tf_op | source)
XLA Modules:
  0.0 99.0 jit_solution(17628554824924413807)
XLA Ops:
  0.6 94.4 %swav_step.1 = (bf16[8,8,16,512]{3,2,1,0:T(8,128)(2,1)S(1)}, bf16[16,32,128]{2,1,0:T(8,128)(2,1)S(1)}, bf16[4,4,2,128,128]{4,3,2,1,0:T(8,128)(2,1)S(1)}) custom-call(bf16[1024,1024]{1,0:T(8,128)(2,1)} %emb_hbm.1, s32[8,128]{1,0:T(8,128)} %bitcast.10, bf16[1024,512]{1,0:T(8,128)(2,1)} %w_in_hbm.1, bf16[512,128]{1,0:T(8,128)(2,1)} %w_out_hbm.1, ...), custom_call_target="tpu_custom_call" | custom-call | tf_op jit(solution)/shard_map/swav_step/pallas_call | solution.py:672
  95.1 1.5 %bitcast_convert_fusion = f32[4096,128]{1,0:T(8,128)} fusion(bf16[4,4,2,128,128]{4,3,2,1,0:T(8,128)(2,1)S(1)} %get-tuple-element.8), kind=kLoop, calls=%fused_computation | loop fusion | flops 524288 | bytes 3145728 | tf_op jit(solution)/shard_map/convert_element_type | solution.py:701
  96.6 1.7 %bitcast_convert_fusion.1 = f32[1024,512]{1,0:T(8,128)} fusion(bf16[8,8,16,512]{3,2,1,0:T(8,128)(2,1)S(1)} %get-tuple-element.6), kind=kLoop, calls=%fused_computation.1 | loop fusion | flops 524288 | bytes 3145728 | tf_op jit(solution)/shard_map/convert_element_type | solution.py:699
  98.3 0.7 bitcast_convert_fusion.2

commit v6 on v5

--- a/solution.py
+++ b/solution.py
@@ -410,6 +410,33 @@
     def _(k):
         raw_copy(k, p).start()
 
+    def second_a(k):
+        return copy(sa_send.at[k], sa_recv.at[k], up_sem.at[2], k, z_peer(k))
+
+    def second_b(k):
+        return copy(sb_send.at[k], sb_recv.at[k], up_sem.at[3], k, y_peer(k))
+
+    @pl.loop(1, 4)
+    def _(k):
+        first_a(k).wait_recv()
+        first_b(k).wait_recv()
+
+    def sum_a(i):
+        return (ua_own[i] + ua_recv[1, i].astype(F32)) + (ua_recv[2, i].astype(F32) + ua_recv[3, i].astype(F32))
+
+    def sum_b(i):
+        return (ub_own[i] + ub_recv[1, i].astype(F32)) + (ub_recv[2, i].astype(F32) + ub_recv[3, i].astype(F32))
+
+    @pl.loop(1, 4)
+    def _(k):
+        sa_send[k] = sum_a(lax.rem(z + k, 4)).astype(BF16)
+        second_a(k).start()
+        sb_send[k] = sum_b(lax.rem(y + k, 4)).astype(BF16)
+        second_b(k).start()
+
+    ua_own[z] = sum_a(z)
+    ub_own[y] = sum_b(y)
+
     @pl.loop(1, NP)
     def _(k):
         raw_copy(k, proto_source(k)).wait_recv()
@@ -446,83 +473,6 @@
     @pl.loop(1, NB)
     def _(k):
         out_copy(k).start()
-
-    def second_a(k):
-        return copy(sa_send.at[k], sa_recv.at[k], up_sem.at[2], k, z_peer(k))
-
-    def second_b(k):
-        return copy(sb_send.at[k], sb_recv.at[k], up_sem.at[3], k, y_peer(k))
-
-    @pl.loop(1, 4)
-    def _(k):
-        first_a(k).wait_recv()
-        first_b(k).wait_recv()
-
-    def sum_a(i):
-        return (ua_own[i] + ua_recv[1, i].astype(F32)) + (ua_recv[2, i].astype(F32) + ua_recv[3, i].astype(F32))
-
-    def sum_b(i):
-        return (ub_own[i] + ub_recv[1, i].astype(F32)) + (ub_recv[2, i].astype(F32) + ub_recv[3, i].astype(F32))
-
-    @pl.loop(1, 4)
-    def _(k):
-        sa_send[k] = sum_a(lax.rem(z + k, 4)).astype(BF16)
-        second_a(k).start()
-        sb_send[k] = sum_b(lax.rem(y + k, 4)).astype(BF16)
-        second_b(k).start()
-
-    ua_own[z] = sum_a(z)
-    ub_own[y] = sum_b(y)
-
-    @pl.loop(1, NB)
-    def _(k):
-        in_copy(k).wait_recv()
-
-    total = gi_f[b // 2, b % 2]
-    for k in range(1, NB):
-        total = total + gi_recv[k].astype(F32)
-    total = total.astype(BF16)
-    gx_send[...] = total
-
-    def tile(q, h):
-        return pl.ds(pl.multiple_of((q % 2 + 2 * h) * 128, 128), 128)
-
-    gin[part_of, b // 2, :, tile(b, 0)] = total[:, :128]
-    gin[part_of, b // 2, :, tile(b, 1)] = total[:, 128:]
-
-    def x_peer(k):
-        return (b, lax.rem(x + k, 4) * 2 + core)
-
-    other_core = (b, x * 2 + 1 - core)
-
-    def a_along_x(k, owner):
-        return copy(gx_send.at[:, pl.ds(0, 128)], gin.at[core * 4 + owner, b // 2, :, tile(b, 0)], ax_sem, k, x_peer(k))
-
-    def b_along_batch(k, q):
-        return copy(gx_send.at[:, pl.ds(128, 128)], gin.at[part_of, q // 2, :, tile(q, 1)], bb_sem, k, batch_peer(k))
-
-    @pl.loop(1, 4)
-    def _(k):
-        a_along_x(k, x).start()
-
-    @pl.loop(1, NB)
-    def _(k):
-        b_along_batch(k, b).start()
-
-    total = go_f[b]
-    for k in range(1, NB):
-        out_copy(k).wait_recv()
-        total = total + go_recv[k].astype(F32)
-    total = total.astype(BF16)
-    goa_send[...] = total
-    gout[b] = total
-
-    def out_all(k, owner):
-        return copy(goa_send, gout.at[owner], goa_sem, k, batch_peer(k))
-
-    @pl.loop(1, NB)
-    def _(k):
-        out_all(k, b).start()
 
     @pl.loop(1, 4)
     def _(k):
@@ -553,6 +503,56 @@
         third_a(k, z).start()
         third_b(k, y).start()
 
+    @pl.loop(1, NB)
+    def _(k):
+        in_copy(k).wait_recv()
+
+    total = gi_f[b // 2, b % 2]
+    for k in range(1, NB):
+        total = total + gi_recv[k].astype(F32)
+    total = total.astype(BF16)
+    gx_send[...] = total
+
+    def tile(q, h):
+        return pl.ds(pl.multiple_of((q % 2 + 2 * h) * 128, 128), 128)
+
+    gin[part_of, b // 2, :, tile(b, 0)] = total[:, :128]
+    gin[part_of, b // 2, :, tile(b, 1)] = total[:, 128:]
+
+    def x_peer(k):
+        return (b, lax.rem(x + k, 4) * 2 + core)
+
+    other_core = (b, x * 2 + 1 - core)
+
+    def a_along_x(k, owner):
+        return copy(gx_send.at[:, pl.ds(0, 128)], gin.at[core * 4 + owner, b // 2, :, tile(b, 0)], ax_sem, k, x_peer(k))
+
+    def b_along_batch(k, q):
+        return copy(gx_send.at[:, pl.ds(128, 128)], gin.at[part_of, q // 2, :, tile(q, 1)], bb_sem, k, batch_peer(k))
+
+    @pl.loop(1, 4)
+    def _(k):
+        a_along_x(k, x).start()
+
+    @pl.loop(1, NB)
+    def _(k):
+        b_along_batch(k, b).start()
+
+    total = go_f[b]
+    for k in range(1, NB):
+        out_copy(k).wait_recv()
+        total = total + go_recv[k].astype(F32)
+    total = total.astype(BF16)
+    goa_send[...] = total
+    gout[b] = total
+
+    def out_all(k, owner):
+        return copy(goa_send, gout.at[owner], goa_sem, k, batch_peer(k))
+
+    @pl.loop(1, NB)
+    def _(k):
+        out_all(k, b).start()
+
     @pl.loop(1, 4)
     def _(k):
         a_along_x(k, back(x, k)).wait_recv()
@@ -573,6 +573,22 @@
 
     a_to_core(0, core).start()
 
+    @pl.loop(1, 4)
+    def _(k):
+        third_a(k, back(z, k)).wait_recv()
+        third_b(k, back(y, k)).wait_recv()
+
+    def fourth_a(k, i):
+        return copy(gproto.at[i, :, 0], gproto.at[i, :, 0], up_sem.at[6], k, y_peer(k))
+
+    def fourth_b(k, i):
+        return copy(gproto.at[:, i, 1], gproto.at[:, i, 1], up_sem.at[7], k, z_peer(k))
+
+    @pl.loop(1, 4)
+    def _(k):
+        fourth_a(k, y).start()
+        fourth_b(k, z).start()
+
     def b_slab(i, c):
         return gin.at[c * 4 + i, :, :, pl.ds(256, 256)]
 
@@ -591,22 +607,6 @@
         b_along_x(k, x).start()
 
     b_to_core(0, core).start()
-
-    @pl.loop(1, 4)
-    def _(k):
-        third_a(k, back(z, k)).wait_recv()
-        third_b(k, back(y, k)).wait_recv()
-
-    def fourth_a(k, i):
-        return copy(gproto.at[i, :, 0], gproto.at[i, :, 0], up_sem.at[6], k, y_peer(k))
-
-    def fourth_b(k, i):
-        return copy(gproto.at[:, i, 1], gproto.at[:, i, 1], up_sem.at[7], k, z_peer(k))
-
-    @pl.loop(1, 4)
-    def _(k):
-        fourth_a(k, y).start()
-        fourth_b(k, z).start()
 
     @pl.loop(1, NB)
     def _(k):

time: 99.2 us -> 98.3 us (level)
  no operation moved by 1% of the time
where the time goes in v6:
time: 98.3 us; the launch traced here: 98.2 us
  Pallas kernels  93.6 us (95%)
  other arithmetic  3.93 us (4%)
    pallas_call x1, Pallas kernels, body(): pl.pallas_call(kernel, name='swav_step', out_shape=(out(NP, 8, 16, H), ou...  93.6 us

profile of v6, /device:TPU:0, one launch (start us, length us, event | category | flops | bytes accessed | tf_op | source)
XLA Modules:
  0.0 98.2 jit_solution(4490078526161830787)
XLA Ops:
  0.6 93.6 %swav_step.1 = (bf16[8,8,16,512]{3,2,1,0:T(8,128)(2,1)S(1)}, bf16[16,32,128]{2,1,0:T(8,128)(2,1)S(1)}, bf16[4,4,2,128,128]{4,3,2,1,0:T(8,128)(2,1)S(1)}) custom-call(bf16[1024,1024]{1,0:T(8,128)(2,1)} %emb_hbm.1, s32[8,128]{1,0:T(8,128)} %bitcast.10, bf16[1024,512]{1,0:T(8,128)(2,1)} %w_in_hbm.1, bf16[512,128]{1,0:T(8,128)(2,1)} %w_out_hbm.1, ...), custom_call_target="tpu_custom_call" | custom-call | tf_op jit(solution)/shard_map/swav_step/pallas_call | solution.py:672
  94.3 1.5 %bitcast_convert_fusion = f32[4096,128]{1,0:T(8,128)} fusion(bf16[4,4,2,128,128]{4,3,2,1,0:T(8,128)(2,1)S(1)} %get-tuple-element.8), kind=kLoop, calls=%fused_computation | loop fusion | flops 524288 | bytes 3145728 | tf_op jit(solution)/shard_map/convert_element_type | solution.py:701
  95.8 1.7 %bitcast_convert_fusion.1 = f32[1024,512]{1,0:T(8,128)} fusion(bf16[8,8,16,512]{3,2,1,0:T(8,128)(2,1)S(1)} %get-tuple-element.6), kind=kLoop, calls=%fused_computation.1 | loop fusion | flops 524288 | bytes 3145728 | tf_op jit(solution)/shard_map/convert_element_type | solution.py:699
  97.5 0.7 bitcast_convert_fusion.2

commit v7 on v6

--- a/solution.py
+++ b/solution.py
@@ -54,7 +54,7 @@
 def kernel(
     emb_hbm, pairing, w_in_hbm, w_out_hbm, proto,
     gin, gout, gproto,
-    emb, w_in, w_out, pre, hidden, raw, perm, perm_t, views, views_t, unit, eh, dsc,
+    emb, w_in, w_out, pre, hidden, raw, perm, perm_t, views, views_t, emb_t, unit, eh, low_d, high_d,
     tot_acc, row_b, row_n, tot_b, raw_own, c_ref,
     col_acc, col_line, col_send, col_recv, row_send, row_recv,
     vun, vg_send, vg_recv, vg_own, dr_send, dr_all, d_raw, d_pre,
@@ -62,9 +62,11 @@
     go_f, go_send, go_recv, goa_send, gi_f, gi_send, gi_recv, gx_send,
     col_sem, row_sem, vg_sem, dr_sem, up_sem, go_sem, goa_sem, gi_sem, ax_sem, ab_sem, ac_sem, bb_sem, bx_sem, bc_sem, in_sem,
 ):
+    dsc = (low_d, high_d)
     b = lax.axis_index("batch")
     p = lax.axis_index("proto")
     x, core = p // 2, p % 2
+    part_of = core * 4 + x
     y, z = b // 4, b % 4
 
     def batch_peer(k):
@@ -210,10 +212,10 @@
 
             def some_rows(i, acc):
                 rows = [pl.ds(pl.multiple_of(i * 64 + m * 16, 16), 16) for m in range(4)]
-                r = [row_n[at, :] for at in rows]
+                r = [row_n[pl.ds(pl.multiple_of(rows_half * 512 + i * 64 + m * 16, 16), 16), :] for m in range(4)]
                 out = []
                 for j, a in zip(lines, acc):
-                    part = pairwise([dsc[rows[m], j * 128 : j * 128 + 128] * r[m] for m in range(4)]).astype(F32)
+                    part = pairwise([dsc[rows_half][rows[m], j * 128 : j * 128 + 128] * r[m] for m in range(4)]).astype(F32)
                     out.append(a + (part[0:8] + part[8:16]))
                 return tuple(out)
 
@@ -221,7 +223,7 @@
                 acc = tuple(jnp.zeros((8, 128), F32) for _ in lines)
             else:
                 acc = tuple(col_acc[:, j * 128 : j * 128 + 128] for j in lines)
-            acc = lax.fori_loop(rows_half * 8, rows_half * 8 + 8, some_rows, acc)
+            acc = lax.fori_loop(0, 8, some_rows, acc)
             if rows_half == 0:
                 for j, a in zip(lines, acc):
                     col_acc[:, j * 128 : j * 128 + 128] = a
@@ -230,26 +232,27 @@
                     col_line[j : j + 1, :] = jnp.sum(a, axis=0, keepdims=True)
                 start_columns(it, h)
 
-    def row_sweep(h, first, last):
+    def row_sweep(h, rows_half):
         lines = range(h * 16, h * 16 + 16)
         c = [jnp.broadcast_to(c_ref[j : j + 1, :], (16, 128)).astype(BF16) for j in lines]
 
-        @pl.loop(first // 16, last // 16)
+        @pl.loop(0, 32)
         def _(i):
-            rows = aligned(i, 16)
+            near, rows = aligned(i, 16), aligned(i + rows_half * 32, 16)
             parts = []
             for g in range(0, 16, 4):
-                some = [dsc[rows, (h * 16 + g + m) * 128 : (h * 16 + g + m + 1) * 128] * c[g + m] for m in range(4)]
+                some = [dsc[rows_half][near, (h * 16 + g + m) * 128 : (h * 16 + g + m + 1) * 128] * c[g + m] for m in range(4)]
                 parts.append(pairwise(some).astype(F32))
             total = pairwise(parts)
             row_b[rows, :] = total if h == 0 else row_b[rows, :] + total
 
     def rows_of(it):
         finish_columns(it, 0)
-        row_sweep(0, 0, R)
+        row_sweep(0, 0)
+        row_sweep(0, 1)
         finish_columns(it, 1)
         for h in range(2):
-            row_sweep(1, h * 512, h * 512 + 512)
+            row_sweep(1, h)
             start_rows(it * 2 + h, row_b, h * 4, 4)
 
     def columns_of(it):
@@ -264,16 +267,15 @@
         cols = aligned(j, 512)
         u = unit[cols, :]
 
-        def some_rows(i, acc):
-            rows = aligned(i, 128)
+        acc = jnp.zeros((8, 512), F32)
+        for i in range(8):
+            rows = slice(i * 128, i * 128 + 128)
             e = jnp.exp2(dot_t(views[rows, :], u) * half_log2)
             eh[rows, cols] = e
             tot_acc[rows, :] += (e[:, 0:128] + e[:, 128:256]) + (e[:, 256:384] + e[:, 384:512])
             e = e * e
-            dsc[rows, cols] = e.astype(BF16)
-            return acc + jnp.sum(e.reshape(16, 8, 512), axis=0)
-
-        acc = lax.fori_loop(0, R // 128, some_rows, jnp.zeros((8, 512), F32), unroll=8)
+            dsc[i // 4][i % 4 * 128 : i % 4 * 128 + 128, cols] = e.astype(BF16)
+            acc = acc + jnp.sum(e.reshape(16, 8, 512), axis=0)
         line = jnp.sum(acc, axis=0, keepdims=True)
         for m in range(4):
             col_line[pl.ds(j * 4 + m, 1), :] = line[:, m * 128 : m * 128 + 128]
@@ -302,6 +304,7 @@
             perm_t[q * 128 : q * 128 + 128, k * 128 : k * 128 + 128] = onehot(at == here)
 
     columns_of(1)
+    emb_t[...] = emb[:, aligned(part_of, 128)].astype(F32).T.astype(BF16)
     own = perm[aligned(p, RC), :]
     r0 = raw[...]
     r1 = r0.astype(BF16)
@@ -317,21 +320,24 @@
     def view_copy(k):
         return copy(vg_send.at[k], vg_recv.at[k], vg_sem, k, proto_peer(k))
 
-    def one_chunk(q):
-        @pl.loop(0, 4)
-        def _(h):
-            top, low = aligned(q * 8 + h, 16), aligned(q * 8 + h + 4, 16)
-            t_top, t_low = tot_b[top, :], tot_b[low, :]
-            r_top, r_low = row_b[top, :], row_b[low, :]
-            for j in range(WV):
-                cols = slice(j * 128, j * 128 + 128)
-                c = c_ref[j : j + 1, :]
-                e_top, e_low = eh[top, cols], eh[low, cols]
-                dsc[top, cols] = (e_top * t_top - (e_low * e_low) * c * r_low).astype(BF16)
-                dsc[low, cols] = (e_low * t_low - (e_top * e_top) * c * r_top).astype(BF16)
-
-        part = dot(dsc[aligned(q, RC), :], unit[...])
-        k = lax.rem(q + NP - p, NP)
+    def some_scores(h, m, part):
+        q = m + h * 4
+        top, low = aligned(q * 8 + part, 16), aligned(q * 8 + part + 4, 16)
+        d_top, d_low = aligned(m * 8 + part, 16), aligned(m * 8 + part + 4, 16)
+        t_top, t_low = tot_b[top, :], tot_b[low, :]
+        r_top, r_low = row_b[top, :], row_b[low, :]
+        for j in range(WV):
+            cols = slice(j * 128, j * 128 + 128)
+            c = c_ref[j : j + 1, :]
+            e_top, e_low = eh[top, cols], eh[low, cols]
+            dsc[h][d_top, cols] = (e_top * t_top - (e_low * e_low) * c * r_low).astype(BF16)
+            dsc[h][d_low, cols] = (e_low * t_low - (e_top * e_top) * c * r_top).astype(BF16)
+
+    def view_part(h, m):
+        return dot(dsc[h][aligned(m, RC), :], unit[...])
+
+    def send_part(h, m, part):
+        k = lax.rem(m + h * 4 + NP - p, NP)
         vg_send[k] = part.astype(BF16)
 
         @pl.when(k > 0)
@@ -342,12 +348,26 @@
         def _():
             vg_own[...] = part
 
-    for h in range(2):
-        spread(finish_rows(2 * ITERS - 2 + h) * loss_gain, row_b, h * 4, 4)
-
-        @pl.loop(1, 5)
-        def _(m):
-            one_chunk(lax.rem(p + m, 4) + h * 4)
+    spread(finish_rows(2 * ITERS - 2) * loss_gain, row_b, 0, 4)
+
+    @pl.loop(0, 16)
+    def _(i):
+        some_scores(0, i // 4, i % 4)
+
+    spread(finish_rows(2 * ITERS - 1) * loss_gain, row_b, 4, 4)
+
+    @pl.loop(1, 5)
+    def _(i):
+        m = lax.rem(p + i, 4)
+        part = view_part(0, m)
+        for n in range(4):
+            some_scores(1, m, n)
+        send_part(0, m, part)
+
+    @pl.loop(1, 5)
+    def _(i):
+        m = lax.rem(p + i, 4)
+        send_part(1, m, view_part(1, m))
 
     def y_peer(k):
         return (lax.rem(y + k, 4) * 4 + z, p)
@@ -369,7 +389,8 @@
         k = lax.rem(kk, 4)
         to_y = lax.rem(y + k, 4)
 
-        parts = dot(views_t[...], dsc[:, aligned(to_y, 4 * CC)])
+        cols = aligned(to_y, 4 * CC)
+        parts = dot(views_t[:, :512], dsc[0][:, cols]) + dot(views_t[:, 512:], dsc[1][:, cols])
         for i in range(4):
             part = parts[:, i * CC : i * CC + CC]
             m = back(i, z)
@@ -448,8 +469,7 @@
         rows = aligned(i, 256)
         d_pre[rows, :] = (pre[rows, :] * dot_t(d_raw[rows, :], w_out[...])).astype(BF16)
 
-    part_of = core * 4 + x
-    gi = dot_tl(emb[:, aligned(part_of, 128)], d_pre[...]).reshape(8, 16, H)
+    gi = dot(emb_t[...], d_pre[...]).reshape(8, 16, H)
     for m in range(2):
         gi_m = jnp.concatenate([gi[:, :, m * 128 : m * 128 + 128], gi[:, :, m * 128 + 256 : m * 128 + 384]], axis=2)
         gi_f[:, m] = gi_m
@@ -677,7 +697,7 @@
         out_specs=(vmem,) * 3,
         scratch_shapes=[
             v((R, E), BF16), v((E, H), BF16), v((H, Z), BF16), v((R, H), F32), v((R, H), BF16), v((R, Z), F32), v((R, R), BF16), v((R, R), BF16),
-            v((R, Z), BF16), v((Z, R), BF16), v((W, Z), BF16), v((R, W), F32), v((R, W), BF16),
+            v((R, Z), BF16), v((Z, R), BF16), v((128, R), BF16), v((W, Z), BF16), v((R, W), F32), v((R // 2, W), BF16), v((R // 2, W), BF16),
             v((R, 128), F32), v((R, 128), F32), v((R, 128), BF16), v((R, 128), F32), v((RC, Z), F32), v((WV, 128), F32),
             v((8, W), F32), v((WV, 128), F32), v((ITERS, 2, 16, 128), BF16), v((ITERS, 2, NB, 16, 128), BF16),
             v((2 * ITERS + 1, 8, 128), F32), v((2 * ITERS + 1, NP, 8, 128), F32),

time: 98.3 us -> 98.2 us (level)
  no operation moved by 1% of the time
where the time goes in v7:
time: 98.2 us; the launch traced here: 98 us
  Pallas kernels  93.4 us (95%)
  other arithmetic  3.93 us (4%)
    pallas_call x1, Pallas kernels, body(): pl.pallas_call(kernel, name='swav_step', out_shape=(out(NP, 8, 16, H), ou...  93.4 us

profile of v7, /device:TPU:0, one launch (start us, length us, event | category | flops | bytes accessed | tf_op | source)
XLA Modules:
  0.0 98.0 jit_solution(12487262699094869155)
XLA Ops:
  0.6 93.4 %swav_step.1 = (bf16[8,8,16,512]{3,2,1,0:T(8,128)(2,1)S(1)}, bf16[16,32,128]{2,1,0:T(8,128)(2,1)S(1)}, bf16[4,4,2,128,128]{4,3,2,1,0:T(8,128)(2,1)S(1)}) custom-call(bf16[1024,1024]{1,0:T(8,128)(2,1)} %emb_hbm.1, s32[8,128]{1,0:T(8,128)} %bitcast.10, bf16[1024,512]{1,0:T(8,128)(2,1)} %w_in_hbm.1, bf16[512,128]{1,0:T(8,128)(2,1)} %w_out_hbm.1, ...), custom_call_target="tpu_custom_call" | custom-call | tf_op jit(solution)/shard_map/swav_step/pallas_call | solution.py:692
  94.1 1.5 %bitcast_convert_fusion = f32[4096,128]{1,0:T(8,128)} fusion(bf16[4,4,2,128,128]{4,3,2,1,0:T(8,128)(2,1)S(1)} %get-tuple-element.8), kind=kLoop, calls=%fused_computation | loop fusion | flops 524288 | bytes 3145728 | tf_op jit(solution)/shard_map/convert_element_type | solution.py:721
  95.6 1.7 %bitcast_convert_fusion.1 = f32[1024,512]{1,0:T(8,128)} fusion(bf16[8,8,16,512]{3,2,1,0:T(8,128)(2,1)S(1)} %get-tuple-element.6), kind=kLoop, calls=%fused_computation.1 | loop fusion | flops 524288 | bytes 3145728 | tf_op jit(solution)/shard_map/convert_element_type | solution.py:719
  97.3 0.7 bitcast_convert_fusion.2

commit v8 on v7

--- a/solution.py
+++ b/solution.py
@@ -280,10 +280,10 @@
         for m in range(4):
             col_line[pl.ds(j * 4 + m, 1), :] = line[:, m * 128 : m * 128 + 128]
 
-    pl.loop(0, 4)(some_columns)
+    pl.loop(0, 5)(some_columns)
     pl.semaphore_wait(barrier, NB - 1 + NP - 1)
     start_columns(0, 0)
-    pl.loop(4, 8)(some_columns)
+    pl.loop(5, 8)(some_columns)
     start_columns(0, 1)
 
     start_rows(2 * ITERS, tot_acc, 0, 8)

time: 98.2 us -> 98 us (level)
  no operation moved by 1% of the time
where the time goes in v8:
time: 98 us; the launch traced here: 97.9 us
  Pallas kernels  93.3 us (95%)
  other arithmetic  3.93 us (4%)
    pallas_call x1, Pallas kernels, body(): pl.pallas_call(kernel, name='swav_step', out_shape=(out(NP, 8, 16, H), ou...  93.3 us

profile of v8, /device:TPU:0, one launch (start us, length us, event | category | flops | bytes accessed | tf_op | source)
XLA Modules:
  0.0 97.9 jit_solution(5344839919716887834)
XLA Ops:
  0.6 93.3 %swav_step.1 = (bf16[8,8,16,512]{3,2,1,0:T(8,128)(2,1)S(1)}, bf16[16,32,128]{2,1,0:T(8,128)(2,1)S(1)}, bf16[4,4,2,128,128]{4,3,2,1,0:T(8,128)(2,1)S(1)}) custom-call(bf16[1024,1024]{1,0:T(8,128)(2,1)} %emb_hbm.1, s32[8,128]{1,0:T(8,128)} %bitcast.10, bf16[1024,512]{1,0:T(8,128)(2,1)} %w_in_hbm.1, bf16[512,128]{1,0:T(8,128)(2,1)} %w_out_hbm.1, ...), custom_call_target="tpu_custom_call" | custom-call | tf_op jit(solution)/shard_map/swav_step/pallas_call | solution.py:692
  94.0 1.5 %bitcast_convert_fusion = f32[4096,128]{1,0:T(8,128)} fusion(bf16[4,4,2,128,128]{4,3,2,1,0:T(8,128)(2,1)S(1)} %get-tuple-element.8), kind=kLoop, calls=%fused_computation | loop fusion | flops 524288 | bytes 3145728 | tf_op jit(solution)/shard_map/convert_element_type | solution.py:721
  95.5 1.7 %bitcast_convert_fusion.1 = f32[1024,512]{1,0:T(8,128)} fusion(bf16[8,8,16,512]{3,2,1,0:T(8,128)(2,1)S(1)} %get-tuple-element.6), kind=kLoop, calls=%fused_computation.1 | loop fusion | flops 524288 | bytes 3145728 | tf_op jit(solution)/shard_map/convert_element_type | solution.py:719
  97.2 0.7 bitcast_convert_fusion.2
